TPU v7x, 32 devices: a whole 2x2x4 slice. The times are simulated.
32 devices in a mesh: tm: 8 (over y, x, core), rows: 4 (over z).
Axes of the slice: x: 2, y: 2, z: 4, core: 2. Of those that a mesh axis runs over, the one named last changes fastest.
Arguments:
- video: bfloat16 [16, 16, 120, 128], P('tm', 'rows'), may hold values from -6 to 6
- norm_gain: bfloat16 [128], replicated, may hold values from 0.099609375 to 1.8984375
- conv_first: bfloat16 [3, 3, 3, 128, 128], replicated, may hold values from -0.109375 to 0.109375
- conv_second: bfloat16 [3, 3, 3, 128, 128], replicated, may hold values from -0.109375 to 0.109375
- attn_gain: bfloat16 [128], replicated, may hold values from 0.099609375 to 1.8984375
- query_weight: bfloat16 [128, 128], replicated, may hold values from -2 to 2
- key_weight: bfloat16 [128, 128], replicated, may hold values from -2 to 2
- value_weight: bfloat16 [128, 128], replicated, may hold values from -0.5 to 0.5
- out_weight: bfloat16 [128, 128], replicated, may hold values from -0.5 to 0.5
Outputs:
- result: bfloat16 [16, 16, 120, 128], P('tm', 'rows')
All inputs are finite; a program needn't handle non-finite values.
Results may differ from a plain program's by a relative error of at most 0.013.
Values may be sent and summed in bfloat16 or wider, within the bound.
No kernel may reach another device: no remote copies, remote signals or barrier semaphores. Data moves between devices by JAX's collectives and lax.ppermute only.
A program may use at most 64 MiB of HBM per device.

v0:
```python
import jax
import jax.numpy as jnp
from jax import lax
from jax.sharding import PartitionSpec as P


def shifted(value, axis, steps):
    count = lax.axis_size(axis)
    leading, last = (max(0, -steps), min(count, count - steps))
    return lax.ppermute(value, axis, [(source, source + steps) for source in range(leading, last)])


def with_halo(x, sides, width):
    for axis, dim in sides:
        size, length = (lax.axis_size(axis), x.shape[dim])
        up = [(i, (i + 1) % size) for i in range(size - 1)]
        down = [(j, i) for i, j in up]
        last = lax.slice_in_dim(x, length - width, length, axis=dim)
        leading = lax.slice_in_dim(x, 0, width, axis=dim)
        before = lax.ppermute(last, axis, up)
        after = lax.ppermute(leading, axis, down)
        x = jnp.concatenate([before, x, after], axis=dim)
    return x


def rms_norm(values, gain):
    wide = values.astype(jnp.float32)
    scale = lax.rsqrt(jnp.mean(wide * wide, axis=-1, keepdims=True) + 1e-06)
    return wide * scale * gain.astype(jnp.float32)


def convolve(field, kernel):
    frames, height, width, chans = field.shape
    earlier = shifted(field, "tm", 1)
    extended = jnp.concatenate([earlier, field], axis=0)
    padded = with_halo(extended, (("rows", 1),), 1)
    padded = jnp.pad(padded, ((0, 0), (0, 0), (1, 1), (0, 0)))
    total = jnp.zeros((frames * height * width, chans), jnp.float32)
    for shift_t in range(3):
        for shift_h in range(3):
            slab = padded[shift_t : shift_t + frames, shift_h : shift_h + height]
            joined = jnp.concatenate([slab[:, :, e : e + width] for e in range(3)], axis=-1)
            taps = kernel[shift_t, shift_h].reshape(3 * chans, chans)
            total = total + jnp.dot(
                joined.reshape(-1, 3 * chans), taps, preferred_element_type=jnp.float32
            )
    return total.reshape(frames, height, width, chans)


def block_scores(query, keys, query_first):
    chans = query.shape[-1]
    scores = jnp.einsum("fpc,gpc->fgp", query, keys, preferred_element_type=jnp.float32) / jnp.sqrt(
        jnp.float32(chans)
    )
    query_pos = query_first + jnp.arange(query.shape[0], dtype=jnp.int32)
    key_pos = jnp.arange(keys.shape[0], dtype=jnp.int32)
    allowed = (key_pos[None, :] <= query_pos[:, None])[:, :, None]
    tile_top = jnp.max(jnp.where(allowed, scores, jnp.float32(-1e30)), axis=1)
    return (scores, allowed, tile_top)


def absorb_block(carry, query, keys, values, query_first):
    top, total, acc = carry
    scores, allowed, tile_top = block_scores(query, keys, query_first)
    new_top = jnp.maximum(top, tile_top)
    weights = jnp.where(allowed, jnp.exp(scores - new_top[:, None, :]), jnp.float32(0.0))
    total = jnp.sum(weights, axis=1)
    update = jnp.einsum(
        "fgp,gpc->fpc", weights.astype(jnp.bfloat16), values, preferred_element_type=jnp.float32
    )
    acc = update
    return (new_top, total, acc)


def start_carry(frames, cells, chans):
    return (
        jnp.full((frames, cells), -1e30, jnp.float32),
        jnp.zeros((frames, cells), jnp.float32),
        jnp.zeros((frames, cells, chans), jnp.float32),
    )


def local(
    video,
    norm_gain,
    conv_first,
    conv_second,
    attn_gain,
    query_weight,
    key_weight,
    value_weight,
    out_weight,
):
    frames, height, width, chans = video.shape
    act = jax.nn.silu(rms_norm(video, norm_gain)).astype(jnp.bfloat16)
    mid = jax.nn.silu(convolve(act, conv_first)).astype(jnp.bfloat16)
    hidden = (video.astype(jnp.float32) + convolve(mid, conv_second)).astype(jnp.bfloat16)
    normed = rms_norm(hidden, attn_gain).astype(jnp.bfloat16)
    flat = normed.reshape(-1, chans)
    joined_weight = jnp.concatenate([query_weight, key_weight, value_weight], axis=1)
    projected = jnp.dot(flat, joined_weight, preferred_element_type=jnp.float32).astype(
        jnp.bfloat16
    )
    cells = height * width
    query = projected[:, :chans].reshape(frames, cells, chans)
    keys = projected[:, chans : 2 * chans].reshape(frames, cells, chans)
    values = projected[:, 2 * chans :].reshape(frames, cells, chans)
    query_first = lax.axis_index("tm") * frames
    top, total, acc = absorb_block(
        start_carry(frames, cells, chans),
        query,
        lax.all_gather(keys, "tm", axis=0, tiled=True),
        lax.all_gather(values, "tm", axis=0, tiled=True),
        query_first,
    )
    mixed = (acc / total[:, :, None]).astype(jnp.bfloat16)
    output = jnp.dot(mixed.reshape(-1, chans), out_weight, preferred_element_type=jnp.float32)
    result = hidden.reshape(-1, chans).astype(jnp.float32) + output
    return result.astype(jnp.bfloat16).reshape(frames, height, width, chans)


def solution(mesh):
    return jax.shard_map(
        local,
        mesh=mesh,
        in_specs=(P("tm", "rows", None, None), P(), P(), P(), P(), P(), P(), P(), P()),
        out_specs=P("tm", "rows", None, None),
        check_vma=False,
    )
```

profile of v0, /device:TPU:0, one launch (start us, length us, event | category | flops | bytes accessed | tf_op | source)
XLA Modules:
  0.0 126.9 jit_solution(13349841878075736519)
XLA Ops:
  6.5 1.2 fusion.26
  7.8 0.7 convert_element_type.47
  8.5 1.2 fusion.33
  9.6 2.4 %collective-permute-start = (bf16[2,4,120,128]{3,2,1,0:T(8,128)(2,1)S(1)}, bf16[2,4,120,128]{3,2,1,0:T(8,128)(2,1)S(1)}, u32[]{:S(2)}, u32[]{:S(2)}) collective-permute-start(bf16[2,4,120,128]{3,2,1,0:T(8,128)(2,1)S(1)} %fusion.33), channel_id=1, source_target_pairs={{0,4},{4,8},{8,12},{12,16},{16,20},{20,24},{24,28},{1,5},{5,9},{9,... | collective-permute-start | bytes 737288 | tf_op jit(solution)/shard_map/ppermute | solution.py:10
  12.1 1.1 collective-permute-done
  13.2 4.3 %collective-permute-start.1 = (bf16[4,1,120,128]{3,2,1,0:T(8,128)(2,1)S(1)}, bf16[4,1,120,128]{3,2,1,0:T(8,128)(2,1)S(1)}, u32[]{:S(2)}, u32[]{:S(2)}) collective-permute-start(bf16[4,1,120,128]{3,2,1,0:T(8,128)(2,1)S(1)} %get-tuple-element.82), channel_id=1, source_target_pairs={{0,1},{1,2},{2,3},{4,5},{5,6},{6,7},{8,9},{9,10},{10,11},{12,13},{... | collective-permute-start | bytes 368648 | tf_op jit(solution)/shard_map/ppermute | solution.py:20
  17.5 1.3 %collective-permute-start.2 = (bf16[4,1,120,128]{3,2,1,0:T(8,128)(2,1)S(1)}, bf16[4,1,120,128]{3,2,1,0:T(8,128)(2,1)S(1)}, u32[]{:S(2)}, u32[]{:S(2)}) collective-permute-start(bf16[4,1,120,128]{3,2,1,0:T(8,128)(2,1)S(1)} %get-tuple-element.83), channel_id=1, source_target_pairs={{1,0},{2,1},{3,2},{5,4},{6,5},{7,6},{9,8},{10,9},{11,10},{13,12},{... | collective-permute-start | bytes 368648 | tf_op jit(solution)/shard_map/ppermute | solution.py:21
  18.9 1.0 collective-permute-done.1
  19.9 4.4 %collective-permute-done.2 = bf16[4,1,120,128]{3,2,1,0:T(8,128)(2,1)S(1)} collective-permute-done((bf16[4,1,120,128]{3,2,1,0:T(8,128)(2,1)S(1)}, bf16[4,1,120,128]{3,2,1,0:T(8,128)(2,1)S(1)}, u32[]{:S(2)}, u32[]{:S(2)}) %collective-permute-start.2) | collective-permute-done | bytes 122912 | tf_op jit(solution)/shard_map/ppermute | solution.py:21
  24.5 0.6 fusion.51
  29.8 4.3 %collective-permute-start.3 = (bf16[2,4,120,128]{3,2,1,0:T(8,128)(2,1)S(1)}, bf16[2,4,120,128]{3,2,1,0:T(8,128)(2,1)S(1)}, u32[]{:S(2)}, u32[]{:S(2)}) collective-permute-start(bf16[2,4,120,128]{3,2,1,0:T(8,128)(2,1)S(1)} %multiply_convert_fusion.1), channel_id=1, source_target_pairs={{0,4},{4,8},{8,12},{12,16},{16,20},{20,24},{24,28},{1,5},{5,9},{9,... | collective-permute-start | bytes 737288 | tf_op jit(solution)/shard_map/ppermute | solution.py:10
  34.1 1.1 collective-permute-done.3
  35.2 3.5 %collective-permute-start.4 = (bf16[4,1,120,128]{3,2,1,0:T(8,128)(2,1)S(1)}, bf16[4,1,120,128]{3,2,1,0:T(8,128)(2,1)S(1)}, u32[]{:S(2)}, u32[]{:S(2)}) collective-permute-start(bf16[4,1,120,128]{3,2,1,0:T(8,128)(2,1)S(1)} %get-tuple-element.78), channel_id=1, source_target_pairs={{0,1},{1,2},{2,3},{4,5},{5,6},{6,7},{8,9},{9,10},{10,11},{12,13},{... | collective-permute-start | bytes 368648 | tf_op jit(solution)/shard_map/ppermute | solution.py:20
  38.7 1.3 %collective-permute-start.5 = (bf16[4,1,120,128]{3,2,1,0:T(8,128)(2,1)S(1)}, bf16[4,1,120,128]{3,2,1,0:T(8,128)(2,1)S(1)}, u32[]{:S(2)}, u32[]{:S(2)}) collective-permute-start(bf16[4,1,120,128]{3,2,1,0:T(8,128)(2,1)S(1)} %get-tuple-element.79), channel_id=1, source_target_pairs={{1,0},{2,1},{3,2},{5,4},{6,5},{7,6},{9,8},{10,9},{11,10},{13,12},{... | collective-permute-start | bytes 368648 | tf_op jit(solution)/shard_map/ppermute | solution.py:21
  40.1 1.0 collective-permute-done.4
  41.1 4.4 %collective-permute-done.5 = bf16[4,1,120,128]{3,2,1,0:T(8,128)(2,1)S(1)} collective-permute-done((bf16[4,1,120,128]{3,2,1,0:T(8,128)(2,1)S(1)}, bf16[4,1,120,128]{3,2,1,0:T(8,128)(2,1)S(1)}, u32[]{:S(2)}, u32[]{:S(2)}) %collective-permute-start.5) | collective-permute-done | bytes 122912 | tf_op jit(solution)/shard_map/ppermute | solution.py:21
  46.0 0.6 fusion.50
  51.9 0.9 fusion.52
  53.7 33.4 %all-gather.5.cloned.1.call-done = bf16[16,480,128]{2,1,0:T(8,128)(2,1)} async-done(((bf16[2,480,128]{2,1,0:T(8,128)(2,1)}), bf16[16,480,128]{2,1,0:T(8,128)(2,1)}) %all-gather.5.cloned.1.call-update) | async-done | bytes 1966096 | tf_op jit(solution)/shard_map/all_gather | solution.py:112
  87.1 2.8 %select_reduce_fusion = (f32[2,480]{0,1:T(8,128)S(1)}, f32[2,16,480]{1,0,2:T(2,128)S(1)}) fusion(pred[2,16]{1,0:T(4,128)(4,1)S(1)} %iota_compare_fusion.2, bf16[2,480,128]{2,1,0:T(8,128)(2,1)S(1)} %bitcast.133, bf16[16,480,128]{2,1,0:T(8,128)(2,1)} %all-gather.5.cloned.1.call-done), kind=kOutput, calls=%fused_computation.81 | convolution fusion | flops 3977280 | bytes 2277152 | tf_op jit(solution)/shard_map/fpc,gpc->fgp/dot_general | solution.py:52
  90.0 1.5 %fusion.44 = f32[2,480]{0,1:T(8,128)S(1)} fusion(f32[2,16,480]{1,0,2:T(2,128)S(1)} %get-tuple-element.91, f32[2,480]{0,1:T(8,128)S(1)} %broadcast_maximum_fusion, pred[2,16]{1,0:T(4,128)(4,1)S(1)} %iota_compare_fusion.2), kind=kLoop, calls=%fused_computation.98 | loop fusion | flops 45120 | bytes 69152 | tf_op jit(solution)/shard_map/reduce_sum | solution.py:67
  91.6 24.6 %all-gather.3.cloned.1.call-done = bf16[16,480,128]{2,1,0:T(8,128)(2,1)} async-done(((bf16[2,480,128]{2,1,0:T(8,128)(2,1)}), bf16[16,480,128]{2,1,0:T(8,128)(2,1)}) %all-gather.3.cloned.1.call-update) | async-done | bytes 1966096 | tf_op jit(solution)/shard_map/all_gather | solution.py:113
  116.3 2.7 %fusion = f32[480,128,2]{1,2,0:T(2,128)S(1)} fusion(bf16[16,480,128]{2,1,0:T(8,128)(2,1)} %all-gather.3.cloned.1.call-done, f32[2,16,480]{1,0,2:T(2,128)S(1)} %get-tuple-element.91, pred[2,16]{1,0:T(4,128)(4,1)S(1)} %iota_compare_fusion.2, f32[2,480]{0,1:T(8,128)S(1)} %broadcast_maximum_fusion), kind=kOutput, calls=%fused_computation.2 | convolution fusion | flops 3978240 | bytes 2522912 | tf_op jit(solution)/shard_map/fgp,gpc->fpc/dot_general | solution.py:68
  119.2 0.9 fusion.11
  (73 shorter events, 11.8 us)
Async XLA Ops:
  6.5 112.6 %copy-start = (bf16[128,128]{1,0:T(8,128)(2,1)S(1)}, bf16[128,128]{1,0:T(8,128)(2,1)}, u32[]{:S(2)}) copy-start(bf16[128,128]{1,0:T(8,128)(2,1)} %param.17) | copy-start | bytes 98308
  6.5 12.3 %copy-start.2 = (bf16[3,3,3,128,128]{4,3,2,1,0:T(8,128)(2,1)S(1)}, bf16[3,3,3,128,128]{4,3,2,1,0:T(8,128)(2,1)}, u32[]{:S(2)}) copy-start(bf16[3,3,3,128,128]{4,3,2,1,0:T(8,128)(2,1)} %param.11) | copy-start | bytes 2654212
  6.5 80.6 %all-gather.5.cloned.1.call-start = ((), (), s32[]{:S(2)}) async-start(), calls=%async_computation.1 | async-start | bytes 2211840 | tf_op jit(solution)/shard_map/all_gather | solution.py:112
  9.6 3.5 %collective-permute-start = (bf16[2,4,120,128]{3,2,1,0:T(8,128)(2,1)S(1)}, bf16[2,4,120,128]{3,2,1,0:T(8,128)(2,1)S(1)}, u32[]{:S(2)}, u32[]{:S(2)}) collective-permute-start(bf16[2,4,120,128]{3,2,1,0:T(8,128)(2,1)S(1)} %fusion.33), channel_id=1, source_target_pairs={{0,4},{4,8},{8,12},{12,16},{16,20},{20,24},{24,28},{1,5},{5,9},{9,... | collective-permute-start | bytes 737288 | tf_op jit(solution)/shard_map/ppermute | solution.py:10
  13.2 6.7 %collective-permute-start.1 = (bf16[4,1,120,128]{3,2,1,0:T(8,128)(2,1)S(1)}, bf16[4,1,120,128]{3,2,1,0:T(8,128)(2,1)S(1)}, u32[]{:S(2)}, u32[]{:S(2)}) collective-permute-start(bf16[4,1,120,128]{3,2,1,0:T(8,128)(2,1)S(1)} %get-tuple-element.82), channel_id=1, source_target_pairs={{0,1},{1,2},{2,3},{4,5},{5,6},{6,7},{8,9},{9,10},{10,11},{12,13},{... | collective-permute-start | bytes 368648 | tf_op jit(solution)/shard_map/ppermute | solution.py:20
  17.5 6.8 %collective-permute-start.2 = (bf16[4,1,120,128]{3,2,1,0:T(8,128)(2,1)S(1)}, bf16[4,1,120,128]{3,2,1,0:T(8,128)(2,1)S(1)}, u32[]{:S(2)}, u32[]{:S(2)}) collective-permute-start(bf16[4,1,120,128]{3,2,1,0:T(8,128)(2,1)S(1)} %get-tuple-element.83), channel_id=1, source_target_pairs={{1,0},{2,1},{3,2},{5,4},{6,5},{7,6},{9,8},{10,9},{11,10},{13,12},{... | collective-permute-start | bytes 368648 | tf_op jit(solution)/shard_map/ppermute | solution.py:21
  29.3 10.7 %copy-start.3 = (bf16[3,3,3,128,128]{4,3,2,1,0:T(8,128)(2,1)S(1)}, bf16[3,3,3,128,128]{4,3,2,1,0:T(8,128)(2,1)}, u32[]{:S(2)}) copy-start(bf16[3,3,3,128,128]{4,3,2,1,0:T(8,128)(2,1)} %param.12) | copy-start | bytes 2654212
  29.6 10.5 %copy-start.7 = (bf16[128]{0:T(256)(128)(2,1)S(1)}, bf16[128]{0:T(256)(128)(2,1)}, u32[]{:S(2)}) copy-start(bf16[128]{0:T(256)(128)(2,1)} %param.13) | copy-start | bytes 772
  29.8 5.4 %collective-permute-start.3 = (bf16[2,4,120,128]{3,2,1,0:T(8,128)(2,1)S(1)}, bf16[2,4,120,128]{3,2,1,0:T(8,128)(2,1)S(1)}, u32[]{:S(2)}, u32[]{:S(2)}) collective-permute-start(bf16[2,4,120,128]{3,2,1,0:T(8,128)(2,1)S(1)} %multiply_convert_fusion.1), channel_id=1, source_target_pairs={{0,4},{4,8},{8,12},{12,16},{16,20},{20,24},{24,28},{1,5},{5,9},{9,... | collective-permute-start | bytes 737288 | tf_op jit(solution)/shard_map/ppermute | solution.py:10
  35.2 5.9 %collective-permute-start.4 = (bf16[4,1,120,128]{3,2,1,0:T(8,128)(2,1)S(1)}, bf16[4,1,120,128]{3,2,1,0:T(8,128)(2,1)S(1)}, u32[]{:S(2)}, u32[]{:S(2)}) collective-permute-start(bf16[4,1,120,128]{3,2,1,0:T(8,128)(2,1)S(1)} %get-tuple-element.78), channel_id=1, source_target_pairs={{0,1},{1,2},{2,3},{4,5},{5,6},{6,7},{8,9},{9,10},{10,11},{12,13},{... | collective-permute-start | bytes 368648 | tf_op jit(solution)/shard_map/ppermute | solution.py:20
  38.7 6.8 %collective-permute-start.5 = (bf16[4,1,120,128]{3,2,1,0:T(8,128)(2,1)S(1)}, bf16[4,1,120,128]{3,2,1,0:T(8,128)(2,1)S(1)}, u32[]{:S(2)}, u32[]{:S(2)}) collective-permute-start(bf16[4,1,120,128]{3,2,1,0:T(8,128)(2,1)S(1)} %get-tuple-element.79), channel_id=1, source_target_pairs={{1,0},{2,1},{3,2},{5,4},{6,5},{7,6},{9,8},{10,9},{11,10},{13,12},{... | collective-permute-start | bytes 368648 | tf_op jit(solution)/shard_map/ppermute | solution.py:21
  50.2 0.9 copy-start.1
  50.5 1.0 copy-start.4
  50.5 1.0 copy-start.5
  50.6 1.0 copy-start.6
  52.9 63.4 %all-gather.3.cloned.1.call-start = ((), (), s32[]{:S(2)}) async-start(), calls=%async_computation | async-start | bytes 2211840 | tf_op jit(solution)/shard_map/all_gather | solution.py:113
Sparse Core Ops, SparseCore 0:
  53.0 34.0 all-gather.4
  89.0 27.2 all-gather.2
where the time goes:
time: 127 us
  waiting for transfers between devices  71.5 us (56%)
  starting transfers between devices  17.3 us (14%)
  between operations  14 us (11%)
  matrix products  13.1 us (10%)
  other arithmetic  8.13 us (6%)
  local copies, waits for them, and re-layouts  2.88 us (2%)
    all_gather x1, waiting for transfers between devices, local(): lax.all_gather(keys, 'tm', axis=0, tiled=True)  33.4 us
    all_gather x1, waiting for transfers between devices, local(): lax.all_gather(values, 'tm', axis=0, tiled=True)  24.6 us
    ppermute x2, waiting for transfers between devices, with_halo(): after = lax.ppermute(leading, axis, down)  8.71 us
    ppermute x2, starting transfers between devices, with_halo(): before = lax.ppermute(last, axis, up)  7.79 us
    ppermute x2, starting transfers between devices, shifted(): lax.ppermute(value, axis, [(source, source + steps) for source in range(l...  6.68 us
    dot_general x18, matrix products, convolve(): jnp.dot(joined.reshape(-1, 3 * chans), taps, preferred_element_type=jnp.f...  6.36 us
    dot_general x1, matrix products, block_scores(): jnp.einsum('fpc,gpc->fgp', query, keys, preferred_element_type=jnp.float32)  2.83 us
    dot_general x1, matrix products, absorb_block(): jnp.einsum('fgp,gpc->fpc', weights.astype(jnp.bfloat16), values, preferre...  2.68 us
  transfers between devices with their start and end apart: 8, of which 8 were waited for; matrix products, arithmetic and copies ran while one was open for 4% of the time, Pallas kernels for 0%

commit v1 on v0

v1 whole, which is shorter than its diff:
```python
import functools

import jax
import jax.numpy as jnp
from jax import lax
from jax.experimental import pallas as pl
from jax.experimental.pallas import tpu as pltpu
from jax.sharding import PartitionSpec as P

F32 = jnp.float32
BF16 = jnp.bfloat16
EPS = 1e-06


def round_up(n, m):
    return (n + m - 1) // m * m


def silu(v):
    return v / (1.0 + jnp.exp(-v))


def rms(v, gain):
    scale = lax.rsqrt(jnp.mean(v * v, axis=-1, keepdims=True) + EPS)
    return v * scale * gain


def lagged(v, steps):
    frame = lax.broadcasted_iota(jnp.int32, v.shape, 0)
    return jnp.where(frame < steps, 0.0, pltpu.roll(v, steps, 0))


def store_taps(dst, row, col, v):
    chans = v.shape[-1]
    for lag in range(3):
        moved = v if lag == 0 else lagged(v, lag)
        dst[row, col, :, lag * chans : (lag + 1) * chans] = moved.astype(BF16)


def build_pair_weight(dst, src):
    chans = src.shape[-1]
    zero = jnp.zeros((chans, chans), BF16)
    for e in range(3):
        for j in range(4):
            for lag in range(3):
                a = 2 - lag
                rows = slice(lag * chans, (lag + 1) * chans)
                dst[e, j, rows, :chans] = src[a, j, e] if j < 3 else zero
                dst[e, j, rows, chans:] = src[a, j - 1, e] if j > 0 else zero


def pair_conv(field, weight, pairs, cols, frames):
    total = None
    depth = field.shape[-1]
    for e in range(3):
        for j in range(4):
            parts = [
                field[2 * p + j, e : e + cols].reshape(cols * frames, depth) for p in range(pairs)
            ]
            lhs = parts[0] if pairs == 1 else jnp.concatenate(parts, axis=0)
            term = jnp.dot(lhs, weight[e, j], preferred_element_type=F32)
            total = term if total is None else total + term
    return total


def block_kernel(
    width,
    height,
    block,
    own_ref,
    above_ref,
    below_ref,
    gain1_ref,
    k1_ref,
    k2_ref,
    gain2_ref,
    wqkv_ref,
    wo_ref,
    out_ref,
    taps1,
    taps2,
    pw1,
    pw2,
    flat,
    raw,
    kept,
    hid,
    qkv,
    res,
):
    frames, rows, wide, chans = own_ref.shape
    first_col = lax.axis_index("tm") * block
    first_row = lax.axis_index("rows") * rows
    gain1 = gain1_ref[...].astype(F32)
    gain2 = gain2_ref[...].astype(F32)

    build_pair_weight(pw1, k1_ref)
    build_pair_weight(pw2, k2_ref)

    for r in range(rows + 4):
        if r < 2:
            x = above_ref[:, r]
        elif r < rows + 2:
            x = own_ref[:, r - 2]
        else:
            x = below_ref[:, r - rows - 2]
        x = x.astype(F32).reshape(frames * wide, chans)
        flat[...] = silu(rms(x, gain1))
        inner = 2 <= r < rows + 2
        if inner:
            raw[...] = x
        for c in range(block + 4):
            v = flat[pl.ds(c, frames, stride=wide), :]
            store_taps(taps1, r, c, v)
            if inner and 2 <= c < block + 2:
                kept[r - 2, c - 2] = raw[pl.ds(c, frames, stride=wide), :]

    cols = block + 2
    pairs = (rows + 2) // 2
    first = pair_conv(taps1, pw1, pairs, cols, frames)
    first = silu(first)
    for p in range(pairs):
        for c in range(cols):
            at = (p * cols + c) * frames
            col = first_col + (c - 1)
            for k in range(2):
                row = first_row + (2 * p + k - 1)
                inside = (col >= 0) & (col < width) & (row >= 0) & (row < height)
                v = first[at : at + frames, k * chans : (k + 1) * chans]
                store_taps(taps2, 2 * p + k, c, jnp.where(inside, v, 0.0))

    pairs = rows // 2
    second = pair_conv(taps2, pw2, pairs, block, frames)
    for p in range(pairs):
        for c in range(block):
            at = (p * block + c) * frames
            for k in range(2):
                r = 2 * p + k
                v = kept[r, c] + second[at : at + frames, k * chans : (k + 1) * chans]
                to = (r * block + c) * frames
                hid[to : to + frames, :] = v.astype(BF16)

    normed = rms(hid[...].astype(F32), gain2).astype(BF16)
    qkv[...] = jnp.dot(normed, wqkv_ref[...], preferred_element_type=F32).astype(BF16)
    count = rows * block * frames
    step = max(128 // frames, 1) * frames
    scale = 1.0 / (float(chans) ** 0.5)
    for lo in range(0, count, step):
        n = min(step, count - lo)
        query = qkv[lo : lo + n, :chans]
        keys = qkv[lo : lo + n, chans : 2 * chans]
        values = qkv[lo : lo + n, 2 * chans :]
        score = lax.dot_general(
            query, keys, (((1,), (1,)), ((), ())), preferred_element_type=F32
        )
        score = score * scale
        i = lax.broadcasted_iota(jnp.int32, (n, n), 0)
        j = lax.broadcasted_iota(jnp.int32, (n, n), 1)
        allowed = (j <= i) & (j >= i - lax.rem(i, frames))
        top = jnp.max(jnp.where(allowed, score, -1e30), axis=-1, keepdims=True)
        terms = jnp.where(allowed, jnp.exp(score - top), 0.0)
        total = jnp.sum(terms, axis=-1, keepdims=True)
        mixed = jnp.dot(terms.astype(BF16), values, preferred_element_type=F32) / total
        out = jnp.dot(mixed.astype(BF16), wo_ref[...], preferred_element_type=F32)
        res[lo : lo + n, :] = hid[lo : lo + n, :].astype(F32) + out

    wide_out = out_ref.shape[2]
    for r in range(rows):
        for c in range(block):
            at = (r * block + c) * frames
            flat[pl.ds(c, frames, stride=wide_out), :] = res[at : at + frames, :]
        back = flat[0 : frames * wide_out, :]
        out_ref[:, r] = back.reshape(frames, wide_out, chans).astype(BF16)


def local(
    width,
    height,
    video,
    norm_gain,
    conv_first,
    conv_second,
    attn_gain,
    query_weight,
    key_weight,
    value_weight,
    out_weight,
):
    few, rows, _, chans = video.shape
    across = lax.axis_size("tm")
    down = lax.axis_size("rows")
    frames = few * across
    block = (width + across - 1) // across
    wide = round_up(block + 4, 8)
    wide_out = round_up(block, 8)

    right = (across - 1) * block + wide - 2 - width
    padded = jnp.pad(video, ((0, 0), (0, 0), (2, right), (0, 0)))
    sent = jnp.stack([padded[:, :, t * block : t * block + wide] for t in range(across)])
    own = lax.all_to_all(sent, "tm", 0, 0, tiled=True).reshape(frames, rows, wide, chans)

    above = lax.ppermute(own[:, rows - 2 :], "rows", [(i, i + 1) for i in range(down - 1)])
    below = lax.ppermute(own[:, :2], "rows", [(i + 1, i) for i in range(down - 1)])

    wqkv = jnp.concatenate([query_weight, key_weight, value_weight], axis=1)
    count = rows * block * frames
    vmem = pl.BlockSpec(memory_space=pltpu.VMEM)
    out = pl.pallas_call(
        functools.partial(block_kernel, width, height, block),
        out_shape=jax.ShapeDtypeStruct((frames, rows, wide_out, chans), BF16),
        in_specs=[vmem] * 9,
        out_specs=vmem,
        scratch_shapes=[
            pltpu.VMEM((rows + 4, block + 4, frames, 3 * chans), BF16),
            pltpu.VMEM((rows + 2, block + 2, frames, 3 * chans), BF16),
            pltpu.VMEM((3, 4, 3 * chans, 2 * chans), BF16),
            pltpu.VMEM((3, 4, 3 * chans, 2 * chans), BF16),
            pltpu.VMEM((frames * wide, chans), F32),
            pltpu.VMEM((frames * wide, chans), F32),
            pltpu.VMEM((rows, block, frames, chans), F32),
            pltpu.VMEM((count, chans), BF16),
            pltpu.VMEM((count, 3 * chans), BF16),
            pltpu.VMEM((count, chans), F32),
        ],
        compiler_params=pltpu.CompilerParams(vmem_limit_bytes=48 << 20),
        name="block",
    )(
        own,
        above,
        below,
        norm_gain.reshape(1, chans),
        conv_first,
        conv_second,
        attn_gain.reshape(1, chans),
        wqkv,
        out_weight,
    )

    sent = out.reshape(across, few, rows, wide_out, chans)
    got = lax.all_to_all(sent, "tm", 0, 0, tiled=True)[:, :, :, :block]
    got = got.transpose(1, 2, 0, 3, 4).reshape(few, rows, across * block, chans)
    return got[:, :, :width]


def solution(mesh):
    spec = P("tm", "rows", None, None)

    def whole(video, *params):
        fn = functools.partial(local, video.shape[2], video.shape[1])
        return jax.shard_map(
            fn, mesh=mesh, in_specs=(spec,) + (P(),) * 8, out_specs=spec, check_vma=False
        )(video, *params)

    return whole
```

time: 127 us -> 47.8 us (0.38)
  waiting for transfers between devices: 71.5 us -> 3.5 us
  blocking collectives: 0 us -> 22.8 us
  between operations: 14 us -> 0.17 us
  matrix products: 13.1 us -> 0 us
  Pallas kernels: 0 us -> 12.4 us
  starting transfers between devices: 17.3 us -> 5.85 us
  other arithmetic: 8.13 us -> 0.02 us
    all_gather x2 -> x0, waiting for transfers between devices: 58.1 us -> none  [the longest x1 33.4 us: local(): lax.all_gather(keys, 'tm', axis=0, tiled=True)]
    all_to_all x0 -> x2, blocking collectives: none -> 22.8 us  [the longest x1 13.4 us: local(): lax.all_to_all(sent, 'tm', 0, 0, tiled=True)]
    dot_general x22 -> x0, matrix products: 13.1 us -> none  [the longest x18 6.36 us: convolve(): jnp.dot(joined.reshape(-1, 3 * chans), taps, preferred_element_type=jnp.f...]
    pallas_call x0 -> x1, Pallas kernels: none -> 12.4 us  [local(): pl.pallas_call(functools.partial(block_kernel, width, height, block), out...]
    ppermute x6 -> x2, starting transfers between devices: 17.1 us -> 5.85 us  [the longest x1 4.56 us: local(): lax.ppermute(own[:, rows - 2:], 'rows', [(i, i + 1) for i in range(down -...]
    ppermute x6 -> x2, waiting for transfers between devices: 13 us -> 3.5 us  [the longest x1 2.32 us: local(): lax.ppermute(own[:, :2], 'rows', [(i + 1, i) for i in range(down - 1)])]
    reduce_sum x3 -> x0, other arithmetic: 2.98 us -> none  [the longest x1 1.51 us: absorb_block(): total = jnp.sum(weights, axis=1)]
    concatenate x15 -> x1, other arithmetic: 2.62 us -> 0.02 us  [local(): wqkv = jnp.concatenate([query_weight, key_weight, value_weight], axis=1)]
  transfers between devices with their start and end apart: 8 -> 2, of which waited for: 8 -> 2; matrix products, arithmetic and copies ran while one was open for 4% -> 0% of each run, Pallas kernels for 0% -> 0%
where the time goes in v1:
time: 47.8 us; the launch traced here: 47.6 us
  blocking collectives  22.8 us (48%)
  Pallas kernels  12.4 us (26%)
  starting transfers between devices  5.85 us (12%)
  waiting for transfers between devices  3.5 us (7%)
  local copies, waits for them, and re-layouts  2.89 us (6%)
    all_to_all x1, blocking collectives, local(): lax.all_to_all(sent, 'tm', 0, 0, tiled=True)  13.4 us
    pallas_call x1, Pallas kernels, local(): pl.pallas_call(functools.partial(block_kernel, width, height, block), out...  12.4 us
    all_to_all x1, blocking collectives, local(): got = lax.all_to_all(sent, 'tm', 0, 0, tiled=True)[:, :, :, :block]  9.32 us
    ppermute x1, starting transfers between devices, local(): lax.ppermute(own[:, rows - 2:], 'rows', [(i, i + 1) for i in range(down -...  4.56 us
    ppermute x1, waiting for transfers between devices, local(): lax.ppermute(own[:, :2], 'rows', [(i + 1, i) for i in range(down - 1)])  2.32 us
    unnamed x25, local copies, waits for them, and re-layouts  1.8 us
    ppermute x1, starting transfers between devices, local(): lax.ppermute(own[:, :2], 'rows', [(i + 1, i) for i in range(down - 1)])  1.29 us
    ppermute x1, waiting for transfers between devices, local(): lax.ppermute(own[:, rows - 2:], 'rows', [(i, i + 1) for i in range(down -...  1.18 us
  transfers between devices with their start and end apart: 2, of which 2 were waited for; matrix products, arithmetic and copies ran while one was open for 0% of the time, Pallas kernels for 0%

profile of v1, /device:TPU:0, one launch (start us, length us, event | category | flops | bytes accessed | tf_op | source)
XLA Modules:
  0.0 47.6 jit_solution(14572699248313133657)
XLA Ops:
  0.0 0.9 %fusion.1 = bf16[8,2,4,24,128]{4,3,2,1,0:T(8,128)(2,1)S(1)} fusion(bf16[2,4,120,128]{3,2,1,0:T(8,128)(2,1)} %param.9), kind=kLoop, calls=%fused_computation.5 | loop fusion | bytes 294912
  0.9 0.1 copy-done.5
  1.1 0.0 copy-start.6
  1.1 0.0 copy-start.7
  1.2 0.0 copy-start.8
  1.2 0.0 copy-start.2
  1.2 0.0 copy-start
  1.2 0.0 copy-start.1
  1.2 13.4 %all_to_all.10 = bf16[8,2,4,24,128]{4,3,2,1,0:T(8,128)(2,1)S(1)} all-to-all(bf16[8,2,4,24,128]{4,3,2,1,0:T(8,128)(2,1)S(1)} %fusion.3), channel_id=1, replica_groups=mesh['tm'=8,'rows'=4] {'tm'}, dimensions={0} | all-to-all | bytes 786432 | tf_op jit(solution)/shard_map/all_to_all | solution.py:200
  14.7 1.3 %collective-permute-start.1 = (bf16[16,2,24,128]{3,2,1,0:T(8,128)(2,1)S(1)}, bf16[16,2,24,128]{3,2,1,0:T(8,128)(2,1)S(1)}, u32[]{:S(2)}, u32[]{:S(2)}) collective-permute-start(bf16[16,2,24,128]{3,2,1,0:T(8,128)(2,1)S(1)} %get-tuple-element.5), channel_id=1, source_target_pairs={{1,0},{2,1},{3,2},{5,4},{6,5},{7,6},{9,8},{10,9},{11,10},{13,12},{... | collective-permute-start | bytes 589832 | tf_op jit(solution)/shard_map/ppermute | solution.py:203
  16.0 4.6 %collective-permute-start = (bf16[16,2,24,128]{3,2,1,0:T(8,128)(2,1)S(1)}, bf16[16,2,24,128]{3,2,1,0:T(8,128)(2,1)S(1)}, u32[]{:S(2)}, u32[]{:S(2)}) collective-permute-start(bf16[16,2,24,128]{3,2,1,0:T(8,128)(2,1)S(1)} %get-tuple-element.6), channel_id=1, source_target_pairs={{0,1},{1,2},{2,3},{4,5},{5,6},{6,7},{8,9},{9,10},{10,11},{12,13},{... | collective-permute-start | bytes 589832 | tf_op jit(solution)/shard_map/ppermute | solution.py:202
  20.6 0.0 copy-done.6
  20.6 0.0 copy-done.7
  20.6 2.3 %collective-permute-done.1.below_ref = bf16[16,2,24,128]{3,2,1,0:T(8,128)(2,1)S(1)} collective-permute-done((bf16[16,2,24,128]{3,2,1,0:T(8,128)(2,1)S(1)}, bf16[16,2,24,128]{3,2,1,0:T(8,128)(2,1)S(1)}, u32[]{:S(2)}, u32[]{:S(2)}) %collective-permute-start.1) | collective-permute-done | bytes 196640 | tf_op jit(solution)/shard_map/ppermute | solution.py:203
  23.0 1.2 %collective-permute-done.above_ref = bf16[16,2,24,128]{3,2,1,0:T(8,128)(2,1)S(1)} collective-permute-done((bf16[16,2,24,128]{3,2,1,0:T(8,128)(2,1)S(1)}, bf16[16,2,24,128]{3,2,1,0:T(8,128)(2,1)S(1)}, u32[]{:S(2)}, u32[]{:S(2)}) %collective-permute-start) | collective-permute-done | bytes 196640 | tf_op jit(solution)/shard_map/ppermute | solution.py:202
  24.1 0.0 copy-done
  24.2 0.6 %copy-done.3 = bf16[128]{0:T(256)(128)(2,1)S(1)} copy-done((bf16[128]{0:T(256)(128)(2,1)S(1)}, bf16[128]{0:T(256)(128)(2,1)}, u32[]{:S(2)}) %copy-start.3) | copy-done | bytes 280
  24.8 0.0 copy-done.4
  24.8 12.4 %block.1 = bf16[16,4,16,128]{3,2,1,0:T(8,128)(2,1)S(1)} custom-call(bf16[16,4,24,128]{3,2,1,0:T(8,128)(2,1)S(1)} %bitcast.28, bf16[16,2,24,128]{3,2,1,0:T(8,128)(2,1)S(1)} %collective-permute-done.above_ref, bf16[16,2,24,128]{3,2,1,0:T(8,128)(2,1)S(1)} %collective-permute-done.1.below_ref, bf16[1,128]{1,0:T(2,128)(2,1)S(1)} %bitcast.30, ...), custom_call_target="tpu_custom_call" | custom-call | tf_op jit(solution)/shard_map/block/pallas_call | solution.py:208
  37.2 0.1 copy.13
  37.3 9.3 %all_to_all.11 = bf16[8,2,4,16,128]{4,2,3,1,0:T(4,128)(2,1)S(1)} all-to-all(bf16[8,2,4,16,128]{4,2,3,1,0:T(4,128)(2,1)S(1)} %copy.13), channel_id=1, replica_groups=mesh['tm'=8,'rows'=4] {'tm'}, dimensions={0} | all-to-all | bytes 524288 | tf_op jit(solution)/shard_map/all_to_all | solution.py:240
  46.7 0.1 slice_bitcast_fusion
  46.7 0.1 copy.14
  46.8 0.7 %copy.15 = bf16[2,4,120,128]{3,2,1,0:T(8,128)(2,1)} copy(bf16[2,4,120,128]{3,1,2,0:T(4,128)(2,1)S(1)} %bitcast.32) | data formatting | bytes 491520 | tf_op jit(solution)/shard_map/reshape | solution.py:241
  (15 shorter events, 0.2 us)
Async XLA Ops:
  0.0 1.0 %copy-start.5 = (bf16[2,4,120,128]{3,2,1,0:T(8,128)(2,1)S(1)}, bf16[2,4,120,128]{3,2,1,0:T(8,128)(2,1)}, u32[]{:S(2)}) copy-start(bf16[2,4,120,128]{3,2,1,0:T(8,128)(2,1)} %param.9) | copy-start | bytes 737284
  1.1 19.4 %copy-start.6 = (bf16[128,128]{1,0:T(8,128)(2,1)S(1)}, bf16[128,128]{1,0:T(8,128)(2,1)}, u32[]{:S(2)}) copy-start(bf16[128,128]{1,0:T(8,128)(2,1)} %param.16) | copy-start | bytes 98308
  1.1 19.4 %copy-start.7 = (bf16[128,128]{1,0:T(8,128)(2,1)S(1)}, bf16[128,128]{1,0:T(8,128)(2,1)}, u32[]{:S(2)}) copy-start(bf16[128,128]{1,0:T(8,128)(2,1)} %param.15) | copy-start | bytes 98308
  1.2 19.4 %copy-start.8 = (bf16[128,128]{1,0:T(8,128)(2,1)S(1)}, bf16[128,128]{1,0:T(8,128)(2,1)}, u32[]{:S(2)}) copy-start(bf16[128,128]{1,0:T(8,128)(2,1)} %param.14) | copy-start | bytes 98308
  1.2 23.0 %copy-start.2 = (bf16[128,128]{1,0:T(8,128)(2,1)S(1)}, bf16[128,128]{1,0:T(8,128)(2,1)}, u32[]{:S(2)}) copy-start(bf16[128,128]{1,0:T(8,128)(2,1)} %wo_ref.1) | copy-start | bytes 98308
  1.2 22.9 %copy-start = (bf16[3,3,3,128,128]{4,3,2,1,0:T(8,128)(2,1)S(1)}, bf16[3,3,3,128,128]{4,3,2,1,0:T(8,128)(2,1)}, u32[]{:S(2)}) copy-start(bf16[3,3,3,128,128]{4,3,2,1,0:T(8,128)(2,1)} %k1_ref.1) | copy-start | bytes 2654212
  1.2 22.9 %copy-start.1 = (bf16[3,3,3,128,128]{4,3,2,1,0:T(8,128)(2,1)S(1)}, bf16[3,3,3,128,128]{4,3,2,1,0:T(8,128)(2,1)}, u32[]{:S(2)}) copy-start(bf16[3,3,3,128,128]{4,3,2,1,0:T(8,128)(2,1)} %k2_ref.1) | copy-start | bytes 2654212
  14.7 8.2 %collective-permute-start.1 = (bf16[16,2,24,128]{3,2,1,0:T(8,128)(2,1)S(1)}, bf16[16,2,24,128]{3,2,1,0:T(8,128)(2,1)S(1)}, u32[]{:S(2)}, u32[]{:S(2)}) collective-permute-start(bf16[16,2,24,128]{3,2,1,0:T(8,128)(2,1)S(1)} %get-tuple-element.5), channel_id=1, source_target_pairs={{1,0},{2,1},{3,2},{5,4},{6,5},{7,6},{9,8},{10,9},{11,10},{13,12},{... | collective-permute-start | bytes 589832 | tf_op jit(solution)/shard_map/ppermute | solution.py:203
  16.0 8.1 %collective-permute-start = (bf16[16,2,24,128]{3,2,1,0:T(8,128)(2,1)S(1)}, bf16[16,2,24,128]{3,2,1,0:T(8,128)(2,1)S(1)}, u32[]{:S(2)}, u32[]{:S(2)}) collective-permute-start(bf16[16,2,24,128]{3,2,1,0:T(8,128)(2,1)S(1)} %get-tuple-element.6), channel_id=1, source_target_pairs={{0,1},{1,2},{2,3},{4,5},{5,6},{6,7},{8,9},{9,10},{10,11},{12,13},{... | collective-permute-start | bytes 589832 | tf_op jit(solution)/shard_map/ppermute | solution.py:202
  24.1 0.7 %copy-start.3 = (bf16[128]{0:T(256)(128)(2,1)S(1)}, bf16[128]{0:T(256)(128)(2,1)}, u32[]{:S(2)}) copy-start(bf16[128]{0:T(256)(128)(2,1)} %param.10) | copy-start | bytes 772
  24.1 0.7 %copy-start.4 = (bf16[128]{0:T(256)(128)(2,1)S(1)}, bf16[128]{0:T(256)(128)(2,1)}, u32[]{:S(2)}) copy-start(bf16[128]{0:T(256)(128)(2,1)} %param.13) | copy-start | bytes 772

commit v2 on v0

v2 whole, which is shorter than its diff:
```python
import functools

import jax
import jax.numpy as jnp
from jax import lax
from jax.experimental import pallas as pl
from jax.experimental.pallas import tpu as pltpu
from jax.sharding import PartitionSpec as P

F32 = jnp.float32
BF16 = jnp.bfloat16
EPS = 1e-06
VMEM = pl.BlockSpec(memory_space=pltpu.VMEM)


def round_up(n, m):
    return (n + m - 1) // m * m


def silu(v):
    half = 0.5 * v
    return half + half * jnp.tanh(half)


def rms(v, gain):
    scale = lax.rsqrt(jnp.mean(v * v, axis=-1, keepdims=True) + EPS)
    return v * scale * gain


class Plan:
    def __init__(self, video, across, width, height):
        self.few, self.rows, _, self.chans = video.shape
        self.across, self.width, self.height = across, width, height
        self.frames = self.few * across
        self.block = (width + across - 1) // across
        self.groups = self.rows // 2
        wide = self.block + 4
        while self.few * 2 * wide % 8:
            wide += 1
        self.wide = wide
        self.stride = 2 * wide
        self.unit = self.few * self.stride
        self.cols = self.block + 2
        self.wide_out = round_up(self.block, 8)
        self.whole_blocks = self.block * across == width


def pack_kernel(plan, video_ref, out_ref, padded, joined):
    lead = 8
    for k in range(plan.few):
        for r in range(plan.rows):
            slot = k * plan.rows + r
            padded[slot, :lead] = jnp.zeros((lead, plan.chans), F32)
            padded[slot, lead : lead + plan.width] = video_ref[k, r].astype(F32)
            tail = padded.shape[1] - lead - plan.width
            padded[slot, lead + plan.width :] = jnp.zeros((tail, plan.chans), F32)
    for t in range(plan.across):
        for g in range(plan.groups):
            slot = (t * plan.groups + g) % joined.shape[0]
            for k in range(plan.few):
                for i in range(2):
                    start = lead - 2 + t * plan.block
                    to = (k * 2 + i) * plan.wide
                    piece = padded[k * plan.rows + 2 * g + i, start : start + plan.wide]
                    joined[slot, to : to + plan.wide] = piece
            out_ref[t, g] = joined[slot].astype(BF16)


def unpack_kernel(plan, got_ref, out_ref, joined):
    for k in range(plan.few):
        for r in range(plan.rows):
            slot = k * plan.rows + r
            for t in range(plan.across):
                at = t * plan.block
                joined[slot, at : at + plan.wide_out] = got_ref[t, k, r].astype(F32)
            out_ref[k, r] = joined[slot, : plan.width].astype(BF16)


def build_pair_weight(dst, src):
    chans = src.shape[-1]
    zero = jnp.zeros((chans, chans), BF16)
    for e in range(3):
        for j in range(4):
            for lag in range(3):
                at = ((j % 2) * 3 + lag) * chans
                for k in range(2):
                    tap = src[2 - lag, j - k, e] if 0 <= j - k <= 2 else zero
                    dst[e, j // 2, at : at + chans, k * chans : (k + 1) * chans] = tap


def act_taps(plan, x, gain, act, dst, g):
    guard = 2 * plan.stride
    act[:guard] = jnp.zeros((guard, plan.chans), F32)
    act[guard:] = silu(rms(x, gain))
    for i in range(2):
        for c in range(plan.block + 4):
            for lag in range(3):
                start = i * plan.wide + c + (2 - lag) * plan.stride
                v = act[pl.ds(start, plan.frames, stride=plan.stride), :]
                at = (i * 3 + lag) * plan.chans
                dst[g, c, :, at : at + plan.chans] = v.astype(BF16)


def half_conv(plan, field, g, weight, half, cols, total=None):
    for e in range(3):
        lhs = field[g, e : e + cols].reshape(cols * plan.frames, field.shape[-1])
        term = jnp.dot(lhs, weight[e, half], preferred_element_type=F32)
        total = term if total is None else total + term
    return total


def mid_taps(plan, total, p, hold, dst, g):
    frames, chans = plan.frames, plan.chans
    first_col = lax.axis_index("tm") * plan.block
    first_row = lax.axis_index("rows") * plan.rows
    mid = silu(total)
    for c in range(plan.cols):
        col = first_col + (c - 1)
        for k in range(2):
            row = first_row + (2 * p + k - 1)
            v = mid[c * frames : (c + 1) * frames, k * chans : (k + 1) * chans]
            edge_col = c in (0, plan.cols - 1) or not plan.whole_blocks
            edge_row = (p == 0 and k == 0) or (p == plan.groups and k == 1)
            if edge_col:
                v = jnp.where((col >= 0) & (col < plan.width), v, 0.0)
            if edge_row:
                v = jnp.where((row >= 0) & (row < plan.height), v, 0.0)
            hold[c, k, :8] = jnp.zeros((8, chans), F32)
            hold[c, k, 8:] = v
            for lag in range(3):
                moved = v if lag == 0 else hold[c, k, 8 - lag : 8 - lag + frames]
                at = (k * 3 + lag) * chans
                dst[g, c, :, at : at + chans] = moved.astype(BF16)


def first_kernel(
    plan,
    own_ref,
    gain_ref,
    k1_ref,
    k2_ref,
    pw1,
    pw2,
    part_ref,
    mid_ref,
    kept_ref,
    taps,
    act,
    raw,
    hold,
):
    gain = gain_ref[...].astype(F32)
    build_pair_weight(pw1, k1_ref)
    for g in range(plan.groups):
        x = own_ref[:, g].astype(F32).reshape(plan.across * plan.unit, plan.chans)
        raw[g] = x
        act_taps(plan, x, gain, act.at[g], taps, g)
        for i in range(2):
            for c in range(plan.block):
                start = i * plan.wide + c + 2
                v = raw[g, pl.ds(start, plan.frames, stride=plan.stride), :]
                kept_ref[2 * g + i, c] = v.astype(BF16)
    part_ref[0] = half_conv(plan, taps, 0, pw1, 1, plan.cols)
    for p in range(1, plan.groups):
        total = half_conv(plan, taps, p - 1, pw1, 0, plan.cols)
        total = half_conv(plan, taps, p, pw1, 1, plan.cols, total)
        mid_taps(plan, total, p, hold, mid_ref, p - 1)
    part_ref[1] = half_conv(plan, taps, plan.groups - 1, pw1, 0, plan.cols)
    build_pair_weight(pw2, k2_ref)


def second_kernel(
    plan,
    above_ref,
    below_ref,
    gain1_ref,
    pw1,
    pw2,
    part_ref,
    mid_ref,
    kept_ref,
    gain2_ref,
    wqkv_ref,
    wo_ref,
    out_ref,
    taps,
    act,
    mid,
    hold,
    hid,
    qkv,
    back,
):
    frames, rows, block, chans = plan.frames, plan.rows, plan.block, plan.chans
    gain1 = gain1_ref[...].astype(F32)
    gain2 = gain2_ref[...].astype(F32)

    totals = []
    for side, ref in enumerate((above_ref, below_ref)):
        x = ref[...].astype(F32).reshape(plan.across * plan.unit, chans)
        act_taps(plan, x, gain1, act.at[side], taps, side)
    for side in range(2):
        totals.append(half_conv(plan, taps, side, pw1, side, plan.cols, part_ref[side]))
    for side in range(2):
        mid_taps(plan, totals[side], side * plan.groups, hold.at[side], mid, side)

    def mid_group(g):
        if g == 0:
            return mid, 0
        return (mid, 1) if g == plan.groups else (mid_ref, g - 1)

    for q in range(plan.groups):
        total = half_conv(plan, *mid_group(q), pw2, 0, block)
        total = half_conv(plan, *mid_group(q + 1), pw2, 1, block, total)
        for k in range(2):
            r = 2 * q + k
            video = kept_ref[r].astype(F32).reshape(block * frames, chans)
            v = video + total[:, k * chans : (k + 1) * chans]
            hid[r * block * frames : (r + 1) * block * frames, :] = v.astype(BF16)

    count = rows * block * frames
    step = max(128 // frames, 1) * frames
    spans = [(lo, min(step, count - lo)) for lo in range(0, count, step)]
    scale = 1.0 / (float(chans) ** 0.5)
    for lo, n in spans:
        normed = rms(hid[lo : lo + n, :].astype(F32), gain2).astype(BF16)
        joined = jnp.dot(normed, wqkv_ref[...], preferred_element_type=F32)
        qkv[lo : lo + n, :] = joined.astype(BF16)
    i = lax.broadcasted_iota(jnp.int32, (step, step), 0)
    j = lax.broadcasted_iota(jnp.int32, (step, step), 1)
    allowed = (j <= i) & (j >= i - lax.rem(i, frames))
    scores = []
    for lo, n in spans:
        score = lax.dot_general(
            qkv[lo : lo + n, :chans],
            qkv[lo : lo + n, chans : 2 * chans],
            (((1,), (1,)), ((), ())),
            preferred_element_type=F32,
        )
        scores.append(jnp.where(allowed[:n, :n], score * scale, -1e30))
    weights = []
    for score in scores:
        top = jnp.max(score, axis=-1, keepdims=True)
        terms = jnp.exp(score - top)
        weights.append((terms.astype(BF16), jnp.sum(terms, axis=-1, keepdims=True)))
    results = []
    for (lo, n), (terms, total) in zip(spans, weights):
        values = qkv[lo : lo + n, 2 * chans :]
        mixed = jnp.dot(terms, values, preferred_element_type=F32) / total
        results.append(mixed.astype(BF16))
    for (lo, n), mixed in zip(spans, results):
        out = jnp.dot(mixed, wo_ref[...], preferred_element_type=F32)
        out = hid[lo : lo + n, :].astype(F32) + out
        for s in range(n // frames):
            r, c = divmod(lo // frames + s, block)
            back[r, pl.ds(c, frames, stride=plan.wide_out), :] = out[s * frames : (s + 1) * frames]

    for r in range(rows):
        out_ref[:, r] = back[r].reshape(frames, plan.wide_out, chans).astype(BF16)


def call(kernel, plan, outs, scratch, operands, name, flops, limit):
    shapes = [jax.ShapeDtypeStruct(s, d) for s, d in outs]
    moved = sum(s.size * s.dtype.itemsize for s in shapes)
    moved += sum(o.size * o.dtype.itemsize for o in operands)
    single = len(shapes) == 1
    return pl.pallas_call(
        functools.partial(kernel, plan),
        out_shape=shapes[0] if single else shapes,
        in_specs=[VMEM] * len(operands),
        out_specs=VMEM if single else [VMEM] * len(shapes),
        scratch_shapes=[pltpu.VMEM(s, d) for s, d in scratch],
        compiler_params=pltpu.CompilerParams(vmem_limit_bytes=limit),
        cost_estimate=pl.CostEstimate(flops=flops, bytes_accessed=moved, transcendentals=0),
        name=name,
    )(*operands)


def local(
    width,
    height,
    video,
    norm_gain,
    conv_first,
    conv_second,
    attn_gain,
    query_weight,
    key_weight,
    value_weight,
    out_weight,
):
    plan = Plan(video, lax.axis_size("tm"), width, height)
    down = lax.axis_size("rows")
    few, rows, groups, chans = plan.few, plan.rows, plan.groups, plan.chans
    across, frames, block, cols = plan.across, plan.frames, plan.block, plan.cols
    gain1 = norm_gain.reshape(1, chans)
    gain2 = attn_gain.reshape(1, chans)

    length = 8 + (across - 1) * block + plan.wide
    sent = call(
        pack_kernel,
        plan,
        [((across, groups, plan.unit, chans), BF16)],
        [((few * rows, round_up(max(length, 8 + width + 8), 8), chans), F32), ((4, plan.unit, chans), F32)],
        (video,),
        "pack",
        0,
        8 << 20,
    )
    own = lax.all_to_all(sent, "tm", 0, 0, tiled=True)

    above = lax.ppermute(own[:, groups - 1], "rows", [(i, i + 1) for i in range(down - 1)])
    below = lax.ppermute(own[:, 0], "rows", [(i + 1, i) for i in range(down - 1)])

    pair = (3, 2, 6 * chans, 2 * chans)
    guarded = (plan.frames + 2) * plan.stride
    pair_flops = 2 * 3 * cols * frames * 6 * chans * 2 * chans
    pw1, pw2, part, inner, kept = call(
        first_kernel,
        plan,
        [
            (pair, BF16),
            (pair, BF16),
            ((2, cols * frames, 2 * chans), F32),
            ((max(groups - 1, 1), cols, frames, 6 * chans), BF16),
            ((rows, block, frames, chans), BF16),
        ],
        [
            ((groups, block + 4, frames, 6 * chans), BF16),
            ((groups, guarded, chans), F32),
            ((groups, across * plan.unit, chans), F32),
            ((cols, 2, frames + 8, chans), F32),
        ],
        (own, gain1, conv_first, conv_second),
        "first",
        pair_flops * 2 * groups,
        24 << 20,
    )

    wqkv = jnp.concatenate([query_weight, key_weight, value_weight], axis=1)
    count = rows * block * frames
    out = call(
        second_kernel,
        plan,
        [((frames, rows, plan.wide_out, chans), BF16)],
        [
            ((2, block + 4, frames, 6 * chans), BF16),
            ((2, guarded, chans), F32),
            ((2, cols, frames, 6 * chans), BF16),
            ((2, cols, 2, frames + 8, chans), F32),
            ((count, chans), BF16),
            ((count, 3 * chans), BF16),
            ((rows, frames * plan.wide_out, chans), F32),
        ],
        (above, below, gain1, pw1, pw2, part, inner, kept, gain2, wqkv, out_weight),
        "second",
        pair_flops * 2 * (groups + 1),
        24 << 20,
    )

    sent = out.reshape(across, few, rows, plan.wide_out, chans)
    got = lax.all_to_all(sent, "tm", 0, 0, tiled=True)
    length = round_up(max((across - 1) * block + plan.wide_out, width), 8)
    return call(
        unpack_kernel,
        plan,
        [((few, rows, width, chans), BF16)],
        [((few * rows, length, chans), F32)],
        (got,),
        "unpack",
        0,
        8 << 20,
    )


def solution(mesh):
    spec = P("tm", "rows", None, None)

    def whole(video, *params):
        fn = functools.partial(local, video.shape[2], video.shape[1])
        return jax.shard_map(
            fn, mesh=mesh, in_specs=(spec,) + (P(),) * 8, out_specs=spec, check_vma=False
        )(video, *params)

    return whole
```

time: 127 us -> 38.6 us (0.30)
  waiting for transfers between devices: 71.5 us -> 0.06 us
  blocking collectives: 0 us -> 21.9 us
  between operations: 14 us -> 0.07 us
  matrix products: 13.1 us -> 0 us
  starting transfers between devices: 17.3 us -> 4.78 us
  other arithmetic: 8.13 us -> 0.81 us
  Pallas kernels: 0 us -> 6.57 us
    all_gather x2 -> x0, waiting for transfers between devices: 58.1 us -> none  [the longest x1 33.4 us: local(): lax.all_gather(keys, 'tm', axis=0, tiled=True)]
    all_to_all x0 -> x2, blocking collectives: none -> 21.9 us  [the longest x1 12.6 us: local(): own = lax.all_to_all(sent, 'tm', 0, 0, tiled=True)]
    dot_general x22 -> x0, matrix products: 13.1 us -> none  [the longest x18 6.36 us: convolve(): jnp.dot(joined.reshape(-1, 3 * chans), taps, preferred_element_type=jnp.f...]
    ppermute x6 -> x2, waiting for transfers between devices: 13 us -> 0.06 us  [the longest x1 0.05 us: local(): lax.ppermute(own[:, 0], 'rows', [(i + 1, i) for i in range(down - 1)])]
    ppermute x6 -> x2, starting transfers between devices: 17.1 us -> 4.78 us  [the longest x1 3.49 us: local(): lax.ppermute(own[:, groups - 1], 'rows', [(i, i + 1) for i in range(down...]
    pallas_call x0 -> x4, Pallas kernels: none -> 6.57 us  [call(): pl.pallas_call(functools.partial(kernel, plan), out_shape=shapes[0] if si...]
    unnamed x16 -> x12, local copies, waits for them, and re-layouts: 0.22 us -> 3.94 us
    reduce_sum x3 -> x0, other arithmetic: 2.98 us -> none  [the longest x1 1.51 us: absorb_block(): total = jnp.sum(weights, axis=1)]
  transfers between devices with their start and end apart: 8 -> 2, of which waited for: 8 -> 1; matrix products, arithmetic and copies ran while one was open for 4% -> 2% of each run, Pallas kernels for 0% -> 6%
where the time goes in v2:
time: 38.6 us; the launch traced here: 38.2 us
  blocking collectives  21.9 us (57%)
  Pallas kernels  6.57 us (17%)
  starting transfers between devices  4.78 us (12%)
  local copies, waits for them, and re-layouts  3.96 us (10%)
  other arithmetic  0.81 us (2%)
    all_to_all x1, blocking collectives, local(): own = lax.all_to_all(sent, 'tm', 0, 0, tiled=True)  12.6 us
    all_to_all x1, blocking collectives, local(): got = lax.all_to_all(sent, 'tm', 0, 0, tiled=True)  9.32 us
    pallas_call x4, Pallas kernels, call(): pl.pallas_call(functools.partial(kernel, plan), out_shape=shapes[0] if si...  6.57 us
    unnamed x12, local copies, waits for them, and re-layouts  3.94 us
    ppermute x1, starting transfers between devices, local(): lax.ppermute(own[:, groups - 1], 'rows', [(i, i + 1) for i in range(down...  3.49 us
    ppermute x1, starting transfers between devices, local(): lax.ppermute(own[:, 0], 'rows', [(i + 1, i) for i in range(down - 1)])  1.29 us
    concatenate x1, other arithmetic, local(): wqkv = jnp.concatenate([query_weight, key_weight, value_weight], axis=1)  0.81 us
  transfers between devices with their start and end apart: 2, of which 1 were waited for; matrix products, arithmetic and copies ran while one was open for 2% of the time, Pallas kernels for 6%

profile of v2, /device:TPU:0, one launch (start us, length us, event | category | flops | bytes accessed | tf_op | source)
XLA Modules:
  0.0 38.2 jit_solution(13365569629683225780)
XLA Ops:
  0.0 0.0 copy-start
  0.0 0.9 %copy-done = bf16[2,4,120,128]{3,2,1,0:T(8,128)(2,1)S(1)} copy-done((bf16[2,4,120,128]{3,2,1,0:T(8,128)(2,1)S(1)}, bf16[2,4,120,128]{3,2,1,0:T(8,128)(2,1)}, u32[]{:S(2)}) %copy-start) | copy-done | bytes 245784
  0.9 0.1 pack.1
  1.1 12.6 %all_to_all.10.own_ref = bf16[8,2,80,128]{3,2,1,0:T(8,128)(2,1)S(1)} all-to-all(bf16[8,2,80,128]{3,2,1,0:T(8,128)(2,1)S(1)} %pack.1), channel_id=1, replica_groups=mesh['tm'=8,'rows'=4] {'tm'}, dimensions={0} | all-to-all | bytes 655360 | tf_op jit(solution)/shard_map/all_to_all | solution.py:310
  13.7 3.5 %collective-permute-start = (bf16[8,80,128]{2,1,0:T(8,128)(2,1)S(1)}, bf16[8,80,128]{2,1,0:T(8,128)(2,1)S(1)}, u32[]{:S(2)}, u32[]{:S(2)}) collective-permute-start(bf16[8,80,128]{2,1,0:T(8,128)(2,1)S(1)} %get-tuple-element.16), channel_id=1, source_target_pairs={{0,1},{1,2},{2,3},{4,5},{5,6},{6,7},{8,9},{9,10},{10,11},{12,13},{... | collective-permute-start | bytes 491528 | tf_op jit(solution)/shard_map/ppermute | solution.py:312
  17.2 1.3 %collective-permute-start.1 = (bf16[8,80,128]{2,1,0:T(8,128)(2,1)S(1)}, bf16[8,80,128]{2,1,0:T(8,128)(2,1)S(1)}, u32[]{:S(2)}, u32[]{:S(2)}) collective-permute-start(bf16[8,80,128]{2,1,0:T(8,128)(2,1)S(1)} %get-tuple-element.15), channel_id=1, source_target_pairs={{1,0},{2,1},{3,2},{5,4},{6,5},{7,6},{9,8},{10,9},{11,10},{13,12},{... | collective-permute-start | bytes 491528 | tf_op jit(solution)/shard_map/ppermute | solution.py:313
  18.5 0.8 %pad_maximum_fusion.wqkv_ref = bf16[128,384]{1,0:T(8,128)(2,1)S(1)} fusion(bf16[128,128]{1,0:T(8,128)(2,1)} %param.16, bf16[128,128]{1,0:T(8,128)(2,1)} %param.15, bf16[128,128]{1,0:T(8,128)(2,1)} %param.14), kind=kLoop, calls=%fused_computation.2 | loop fusion | flops 294912 | bytes 196608 | tf_op jit(solution)/shard_map/concatenate | solution.py:340
  19.3 0.0 copy-start.1
  19.3 1.2 %copy-done.1 = bf16[3,3,3,128,128]{4,3,2,1,0:T(8,128)(2,1)S(1)} copy-done((bf16[3,3,3,128,128]{4,3,2,1,0:T(8,128)(2,1)S(1)}, bf16[3,3,3,128,128]{4,3,2,1,0:T(8,128)(2,1)}, u32[]{:S(2)}) %copy-start.1) | copy-done | bytes 884760
  20.5 0.0 copy-start.2
  20.5 1.2 %copy-done.2 = bf16[3,3,3,128,128]{4,3,2,1,0:T(8,128)(2,1)S(1)} copy-done((bf16[3,3,3,128,128]{4,3,2,1,0:T(8,128)(2,1)S(1)}, bf16[3,3,3,128,128]{4,3,2,1,0:T(8,128)(2,1)}, u32[]{:S(2)}) %copy-start.2) | copy-done | bytes 884760
  21.6 0.0 copy-start.4
  21.7 0.7 %copy-done.4 = bf16[128]{0:T(256)(128)(2,1)S(1)} copy-done((bf16[128]{0:T(256)(128)(2,1)S(1)}, bf16[128]{0:T(256)(128)(2,1)}, u32[]{:S(2)}) %copy-start.4) | copy-done | bytes 280
  22.3 0.0 copy-start.3
  22.3 0.0 copy-start.5
  22.3 2.3 %first.1 = (bf16[3,2,768,256]{3,2,1,0:T(8,128)(2,1)S(1)}, bf16[3,2,768,256]{3,2,1,0:T(8,128)(2,1)S(1)}, f32[2,272,256]{2,1,0:T(8,128)S(1)}, bf16[1,17,16,768]{3,...) custom-call(bf16[8,2,80,128]{3,2,1,0:T(8,128)(2,1)S(1)} %all_to_all.10.own_ref, bf16[1,128]{1,0:T(2,128)(2,1)S(1)} %bitcast.12, ...), custom_call_target="tpu_custom_call" | custom-call | flops 1283457024 | bytes 8036608 | tf_op jit(solution)/shard_map/first/pallas_call | solution.py:267
  24.6 0.0 collective-permute-done.above_ref
  24.6 0.1 collective-permute-done.1.below_ref
  24.7 0.0 copy-done.3
  24.7 0.0 copy-done.5
  24.7 3.4 %second.1 = bf16[16,4,16,128]{3,2,1,0:T(8,128)(2,1)S(1)} custom-call(bf16[8,80,128]{2,1,0:T(8,128)(2,1)S(1)} %collective-permute-done.above_ref, bf16[8,80,128]{2,1,0:T(8,128)(2,1)S(1)} %collective-permute-done.1.below_ref, bf16[1,128]{1,0:T(2,128)(2,1)S(1)} %bitcast.13, bf16[3,2,768,256]{3,2,1,0:T(8,128)(2,1)S(1)} %get-tuple-element.10.pw1, ...), custom_call_target="tpu_custom_call" | custom-call | flops 1925185536 | bytes 6660608 | tf_op jit(solution)/shard_map/second/pallas_call | solution.py:267
  28.1 9.3 %all_to_all.11.got_ref = bf16[8,2,4,16,128]{4,3,2,1,0:T(8,128)(2,1)S(1)} all-to-all(bf16[8,2,4,16,128]{4,3,2,1,0:T(8,128)(2,1)S(1)} %bitcast.11), channel_id=1, replica_groups=mesh['tm'=8,'rows'=4] {'tm'}, dimensions={0} | all-to-all | bytes 524288 | tf_op jit(solution)/shard_map/all_to_all | solution.py:362
  37.4 0.8 %unpack.1 = bf16[2,4,120,128]{3,2,1,0:T(8,128)(2,1)} custom-call(bf16[8,2,4,16,128]{4,3,2,1,0:T(8,128)(2,1)S(1)} %all_to_all.11.got_ref), custom_call_target="tpu_custom_call" | custom-call | bytes 507904 | tf_op jit(solution)/shard_map/unpack/pallas_call | solution.py:267
  (1 shorter events, 0.0 us)
Async XLA Ops:
  0.0 0.9 %copy-start = (bf16[2,4,120,128]{3,2,1,0:T(8,128)(2,1)S(1)}, bf16[2,4,120,128]{3,2,1,0:T(8,128)(2,1)}, u32[]{:S(2)}) copy-start(bf16[2,4,120,128]{3,2,1,0:T(8,128)(2,1)} %video_ref.1) | copy-start | bytes 737284
  13.7 10.9 %collective-permute-start = (bf16[8,80,128]{2,1,0:T(8,128)(2,1)S(1)}, bf16[8,80,128]{2,1,0:T(8,128)(2,1)S(1)}, u32[]{:S(2)}, u32[]{:S(2)}) collective-permute-start(bf16[8,80,128]{2,1,0:T(8,128)(2,1)S(1)} %get-tuple-element.16), channel_id=1, source_target_pairs={{0,1},{1,2},{2,3},{4,5},{5,6},{6,7},{8,9},{9,10},{10,11},{12,13},{... | collective-permute-start | bytes 491528 | tf_op jit(solution)/shard_map/ppermute | solution.py:312
  17.2 7.5 %collective-permute-start.1 = (bf16[8,80,128]{2,1,0:T(8,128)(2,1)S(1)}, bf16[8,80,128]{2,1,0:T(8,128)(2,1)S(1)}, u32[]{:S(2)}, u32[]{:S(2)}) collective-permute-start(bf16[8,80,128]{2,1,0:T(8,128)(2,1)S(1)} %get-tuple-element.15), channel_id=1, source_target_pairs={{1,0},{2,1},{3,2},{5,4},{6,5},{7,6},{9,8},{10,9},{11,10},{13,12},{... | collective-permute-start | bytes 491528 | tf_op jit(solution)/shard_map/ppermute | solution.py:313
  19.3 1.2 %copy-start.1 = (bf16[3,3,3,128,128]{4,3,2,1,0:T(8,128)(2,1)S(1)}, bf16[3,3,3,128,128]{4,3,2,1,0:T(8,128)(2,1)}, u32[]{:S(2)}) copy-start(bf16[3,3,3,128,128]{4,3,2,1,0:T(8,128)(2,1)} %k1_ref.1) | copy-start | bytes 2654212
  20.5 1.2 %copy-start.2 = (bf16[3,3,3,128,128]{4,3,2,1,0:T(8,128)(2,1)S(1)}, bf16[3,3,3,128,128]{4,3,2,1,0:T(8,128)(2,1)}, u32[]{:S(2)}) copy-start(bf16[3,3,3,128,128]{4,3,2,1,0:T(8,128)(2,1)} %k2_ref.1) | copy-start | bytes 2654212
  21.6 0.7 %copy-start.4 = (bf16[128]{0:T(256)(128)(2,1)S(1)}, bf16[128]{0:T(256)(128)(2,1)}, u32[]{:S(2)}) copy-start(bf16[128]{0:T(256)(128)(2,1)} %param.10) | copy-start | bytes 772
  22.3 2.4 %copy-start.3 = (bf16[128,128]{1,0:T(8,128)(2,1)S(1)}, bf16[128,128]{1,0:T(8,128)(2,1)}, u32[]{:S(2)}) copy-start(bf16[128,128]{1,0:T(8,128)(2,1)} %wo_ref.1) | copy-start | bytes 98308
  22.3 2.4 %copy-start.5 = (bf16[128]{0:T(256)(128)(2,1)S(1)}, bf16[128]{0:T(256)(128)(2,1)}, u32[]{:S(2)}) copy-start(bf16[128]{0:T(256)(128)(2,1)} %param.13) | copy-start | bytes 772

commit v3 on v2

--- a/solution.py
+++ b/solution.py
@@ -34,6 +34,7 @@
         self.frames = self.few * across
         self.block = (width + across - 1) // across
         self.groups = self.rows // 2
+        self.chips = across // 2
         wide = self.block + 4
         while self.few * 2 * wide % 8:
             wide += 1
@@ -45,8 +46,10 @@
         self.whole_blocks = self.block * across == width
 
 
-def pack_kernel(plan, video_ref, out_ref, padded, joined):
+def pack_kernel(plan, s, video_ref, *refs):
+    outs, (padded, joined) = refs[-plan.chips - 2 : -2], refs[-2:]
     lead = 8
+    me = lax.axis_index("tm")
     for k in range(plan.few):
         for r in range(plan.rows):
             slot = k * plan.rows + r
@@ -54,26 +57,46 @@
             padded[slot, lead : lead + plan.width] = video_ref[k, r].astype(F32)
             tail = padded.shape[1] - lead - plan.width
             padded[slot, lead + plan.width :] = jnp.zeros((tail, plan.chans), F32)
-    for t in range(plan.across):
+    for d in range(plan.chips):
+        start = lead - 2 + jnp.bitwise_xor(me, 2 * d) * plan.block
         for g in range(plan.groups):
-            slot = (t * plan.groups + g) % joined.shape[0]
+            at = (d * plan.groups + g) % joined.shape[0]
             for k in range(plan.few):
                 for i in range(2):
-                    start = lead - 2 + t * plan.block
+                    slot = k * plan.rows + 2 * g + i
                     to = (k * 2 + i) * plan.wide
-                    piece = padded[k * plan.rows + 2 * g + i, start : start + plan.wide]
-                    joined[slot, to : to + plan.wide] = piece
-            out_ref[t, g] = joined[slot].astype(BF16)
-
-
-def unpack_kernel(plan, got_ref, out_ref, joined):
+                    joined[at, to : to + plan.wide] = padded[slot, pl.ds(start, plan.wide)]
+            outs[d][g, s] = joined[at].astype(BF16)
+
+
+def unpack_kernel(plan, *refs):
+    gots, rec_ref, out_ref, joined = refs[: plan.chips], *refs[plan.chips :]
+    me = lax.axis_index("tm")
     for k in range(plan.few):
         for r in range(plan.rows):
             slot = k * plan.rows + r
-            for t in range(plan.across):
-                at = t * plan.block
-                joined[slot, at : at + plan.wide_out] = got_ref[t, k, r].astype(F32)
+            for d in range(plan.chips):
+                for s in range(2):
+                    at = jnp.bitwise_xor(me, 2 * d + s) * plan.block
+                    part = rec_ref[d, k, r] if s else gots[d][0, k, r]
+                    joined[slot, pl.ds(at, plan.block)] = part.astype(F32)[: plan.block]
             out_ref[k, r] = joined[slot, : plan.width].astype(BF16)
+
+
+def prep_kernel(plan, *refs):
+    sources, (pw1, pw2, wqkv, k1, k2, sems) = refs[:5], refs[5:]
+    chans = plan.chans
+    targets = [k1, k2] + [wqkv.at[:, i * chans : (i + 1) * chans] for i in range(3)]
+    copies = []
+    for i, (source, target) in enumerate(zip(sources, targets)):
+        copies.append(pltpu.make_async_copy(source, target, sems.at[i]))
+        copies[i].start()
+    copies[0].wait()
+    build_pair_weight(pw1, k1)
+    copies[1].wait()
+    build_pair_weight(pw2, k2)
+    for copy in copies[2:]:
+        copy.wait()
 
 
 def build_pair_weight(dst, src):
@@ -101,9 +124,20 @@
                 dst[g, c, :, at : at + plan.chans] = v.astype(BF16)
 
 
-def half_conv(plan, field, g, weight, half, cols, total=None):
+def in_order(plan, pieces, raw):
+    me = lax.axis_index("tm")
+    for i in range(plan.across):
+        to = pl.multiple_of(jnp.bitwise_xor(me, i) * plan.unit, 8)
+        raw[pl.ds(to, plan.unit), :] = pieces(i).astype(F32)
+
+
+def half_conv(plan, parts, weight, half, cols, total=None):
     for e in range(3):
-        lhs = field[g, e : e + cols].reshape(cols * plan.frames, field.shape[-1])
+        lhs = [
+            f[g : g + n, e : e + cols].reshape(n * cols * plan.frames, f.shape[-1])
+            for f, g, n in parts
+        ]
+        lhs = lhs[0] if len(lhs) == 1 else jnp.concatenate(lhs, axis=0)
         term = jnp.dot(lhs, weight[e, half], preferred_element_type=F32)
         total = term if total is None else total + term
     return total
@@ -133,92 +167,63 @@
                 dst[g, c, :, at : at + chans] = moved.astype(BF16)
 
 
-def first_kernel(
-    plan,
-    own_ref,
-    gain_ref,
-    k1_ref,
-    k2_ref,
-    pw1,
-    pw2,
-    part_ref,
-    mid_ref,
-    kept_ref,
-    taps,
-    act,
-    raw,
-    hold,
-):
+def first_kernel(plan, *refs):
+    pieces, refs = refs[: plan.chips], refs[plan.chips :]
+    gain_ref, pw1, part_ref, mid_ref, kept_ref, taps, act, raw, hold = refs
     gain = gain_ref[...].astype(F32)
-    build_pair_weight(pw1, k1_ref)
     for g in range(plan.groups):
-        x = own_ref[:, g].astype(F32).reshape(plan.across * plan.unit, plan.chans)
-        raw[g] = x
-        act_taps(plan, x, gain, act.at[g], taps, g)
+        in_order(plan, lambda i: pieces[i // 2][g, i % 2], raw.at[g])
+        act_taps(plan, raw[g], gain, act.at[g], taps, g)
         for i in range(2):
             for c in range(plan.block):
                 start = i * plan.wide + c + 2
                 v = raw[g, pl.ds(start, plan.frames, stride=plan.stride), :]
                 kept_ref[2 * g + i, c] = v.astype(BF16)
-    part_ref[0] = half_conv(plan, taps, 0, pw1, 1, plan.cols)
+    lower = half_conv(plan, [(taps, 0, plan.groups)], pw1, 0, plan.cols)
+    upper = half_conv(plan, [(taps, 0, plan.groups)], pw1, 1, plan.cols)
+    size = plan.cols * plan.frames
+    part_ref[0] = upper[:size]
     for p in range(1, plan.groups):
-        total = half_conv(plan, taps, p - 1, pw1, 0, plan.cols)
-        total = half_conv(plan, taps, p, pw1, 1, plan.cols, total)
+        total = lower[(p - 1) * size : p * size] + upper[p * size : (p + 1) * size]
         mid_taps(plan, total, p, hold, mid_ref, p - 1)
-    part_ref[1] = half_conv(plan, taps, plan.groups - 1, pw1, 0, plan.cols)
-    build_pair_weight(pw2, k2_ref)
-
-
-def second_kernel(
-    plan,
-    above_ref,
-    below_ref,
-    gain1_ref,
-    pw1,
-    pw2,
-    part_ref,
-    mid_ref,
-    kept_ref,
-    gain2_ref,
-    wqkv_ref,
-    wo_ref,
-    out_ref,
-    taps,
-    act,
-    mid,
-    hold,
-    hid,
-    qkv,
-    back,
-):
+    part_ref[1] = lower[(plan.groups - 1) * size :]
+
+
+def second_kernel(plan, *refs):
+    sides, refs = refs[:2], refs[2:]
+    gain1_ref, pw1, pw2, part_ref, mid_ref, kept_ref, gain2_ref, wqkv_ref, wo_ref = refs[:9]
+    outs, refs = refs[9 : 9 + plan.chips], refs[9 + plan.chips :]
+    taps, act, raw, mid, hold, hid, qkv, back = refs
     frames, rows, block, chans = plan.frames, plan.rows, plan.block, plan.chans
     gain1 = gain1_ref[...].astype(F32)
     gain2 = gain2_ref[...].astype(F32)
 
     totals = []
-    for side, ref in enumerate((above_ref, below_ref)):
-        x = ref[...].astype(F32).reshape(plan.across * plan.unit, chans)
-        act_taps(plan, x, gain1, act.at[side], taps, side)
+    for side, ref in enumerate(sides):
+        in_order(plan, lambda i: ref[i], raw.at[side])
+        act_taps(plan, raw[side], gain1, act.at[side], taps, side)
     for side in range(2):
-        totals.append(half_conv(plan, taps, side, pw1, side, plan.cols, part_ref[side]))
+        total = half_conv(plan, [(taps, side, 1)], pw1, side, plan.cols)
+        totals.append(total + part_ref[side])
     for side in range(2):
         mid_taps(plan, totals[side], side * plan.groups, hold.at[side], mid, side)
 
     def mid_group(g):
         if g == 0:
-            return mid, 0
-        return (mid, 1) if g == plan.groups else (mid_ref, g - 1)
-
+            return [(mid, 0, 1)]
+        return [(mid, 1, 1)] if g == plan.groups else [(mid_ref, g - 1, 1)]
+
+    size = block * frames
     for q in range(plan.groups):
-        total = half_conv(plan, *mid_group(q), pw2, 0, block)
-        total = half_conv(plan, *mid_group(q + 1), pw2, 1, block, total)
+        total = half_conv(plan, mid_group(q), pw2, 0, block)
+        total = half_conv(plan, mid_group(q + 1), pw2, 1, block, total)
         for k in range(2):
             r = 2 * q + k
-            video = kept_ref[r].astype(F32).reshape(block * frames, chans)
+            video = kept_ref[r].astype(F32).reshape(size, chans)
             v = video + total[:, k * chans : (k + 1) * chans]
-            hid[r * block * frames : (r + 1) * block * frames, :] = v.astype(BF16)
-
-    count = rows * block * frames
+            hid[r * size : (r + 1) * size, :] = v.astype(BF16)
+
+    count = rows * size
     step = max(128 // frames, 1) * frames
     spans = [(lo, min(step, count - lo)) for lo in range(0, count, step)]
     scale = 1.0 / (float(chans) ** 0.5)
@@ -253,27 +258,41 @@
         out = hid[lo : lo + n, :].astype(F32) + out
         for s in range(n // frames):
             r, c = divmod(lo // frames + s, block)
-            back[r, pl.ds(c, frames, stride=plan.wide_out), :] = out[s * frames : (s + 1) * frames]
-
-    for r in range(rows):
-        out_ref[:, r] = back[r].reshape(frames, plan.wide_out, chans).astype(BF16)
-
-
-def call(kernel, plan, outs, scratch, operands, name, flops, limit):
+            v = out[s * frames : (s + 1) * frames]
+            back[r, pl.ds(c, frames, stride=plan.wide_out), :] = v
+
+    me = lax.axis_index("tm")
+    for d in range(plan.chips):
+        for s in range(2):
+            owner = jnp.bitwise_xor(me, 2 * d + s)
+            span = plan.few * plan.wide_out
+            for r in range(rows):
+                v = back[r, pl.ds(pl.multiple_of(owner * span, 8), span), :]
+                v = v.reshape(plan.few, plan.wide_out, chans)
+                outs[d][s, :, r] = v.astype(BF16)
+
+
+def call(kernel, outs, scratch, operands, name, flops, limit, specs=None, aliases=None):
     shapes = [jax.ShapeDtypeStruct(s, d) for s, d in outs]
-    moved = sum(s.size * s.dtype.itemsize for s in shapes)
-    moved += sum(o.size * o.dtype.itemsize for o in operands)
+    moved = sum(s.size * s.dtype.itemsize for s in shapes) if flops else 0
     single = len(shapes) == 1
+    scratch = [pltpu.VMEM(*s) if isinstance(s, tuple) else s for s in scratch]
     return pl.pallas_call(
-        functools.partial(kernel, plan),
+        kernel,
         out_shape=shapes[0] if single else shapes,
-        in_specs=[VMEM] * len(operands),
+        in_specs=specs or [VMEM] * len(operands),
         out_specs=VMEM if single else [VMEM] * len(shapes),
-        scratch_shapes=[pltpu.VMEM(s, d) for s, d in scratch],
+        scratch_shapes=scratch,
+        input_output_aliases=aliases or {},
         compiler_params=pltpu.CompilerParams(vmem_limit_bytes=limit),
         cost_estimate=pl.CostEstimate(flops=flops, bytes_accessed=moved, transcendentals=0),
         name=name,
     )(*operands)
+
+
+def exchange(value, distance):
+    size = lax.axis_size("tm")
+    return lax.ppermute(value, "tm", [(i, i ^ distance) for i in range(size)])
 
 
 def local(
@@ -293,34 +312,53 @@
     down = lax.axis_size("rows")
     few, rows, groups, chans = plan.few, plan.rows, plan.groups, plan.chans
     across, frames, block, cols = plan.across, plan.frames, plan.block, plan.cols
+    chips, unit = plan.chips, plan.unit
     gain1 = norm_gain.reshape(1, chans)
     gain2 = attn_gain.reshape(1, chans)
 
-    length = 8 + (across - 1) * block + plan.wide
-    sent = call(
-        pack_kernel,
-        plan,
-        [((across, groups, plan.unit, chans), BF16)],
-        [((few * rows, round_up(max(length, 8 + width + 8), 8), chans), F32), ((4, plan.unit, chans), F32)],
-        (video,),
-        "pack",
+    other = exchange(video, 1)
+    length = round_up(max(8 + (across - 1) * block + plan.wide, 8 + width + 8), 8)
+    pieces = ()
+    for s, value in enumerate((video, other)):
+        pieces = call(
+            functools.partial(pack_kernel, plan, s),
+            [((groups, 2, unit, chans), BF16)] * chips,
+            [((few * rows, length, chans), F32), ((4, unit, chans), F32)],
+            (value, *pieces),
+            ("pack_own", "pack_other")[s],
+            0,
+            4 << 20,
+            aliases={1 + d: d for d in range(chips)} if s else None,
+            specs=[VMEM] + [pl.BlockSpec(memory_space=pl.ANY)] * (chips if s else 0),
+        )
+    pieces = [pieces[0]] + [exchange(pieces[d], 2 * d) for d in range(1, chips)]
+
+    pair = (3, 2, 6 * chans, 2 * chans)
+    pair_flops = 2 * 3 * cols * frames * 6 * chans * 2 * chans
+    prepared = call(
+        functools.partial(prep_kernel, plan),
+        [(pair, BF16), (pair, BF16), ((chans, 3 * chans), BF16)],
+        [(conv_first.shape, BF16), (conv_second.shape, BF16), pltpu.SemaphoreType.DMA((5,))],
+        [
+            pltpu.with_memory_space_constraint(w, pltpu.HBM)
+            for w in (conv_first, conv_second, query_weight, key_weight, value_weight)
+        ],
+        "prep",
         0,
-        8 << 20,
+        4 << 20,
+        specs=[pl.BlockSpec(memory_space=pltpu.HBM)] * 5,
     )
-    own = lax.all_to_all(sent, "tm", 0, 0, tiled=True)
-
-    above = lax.ppermute(own[:, groups - 1], "rows", [(i, i + 1) for i in range(down - 1)])
-    below = lax.ppermute(own[:, 0], "rows", [(i + 1, i) for i in range(down - 1)])
-
-    pair = (3, 2, 6 * chans, 2 * chans)
-    guarded = (plan.frames + 2) * plan.stride
-    pair_flops = 2 * 3 * cols * frames * 6 * chans * 2 * chans
-    pw1, pw2, part, inner, kept = call(
-        first_kernel,
-        plan,
+    pieces, (pw1, pw2, wqkv) = lax.optimization_barrier((pieces, prepared))
+
+    upward = jnp.concatenate([p[groups - 1] for p in pieces])
+    downward = jnp.concatenate([p[0] for p in pieces])
+    above = lax.ppermute(upward, "rows", [(i, i + 1) for i in range(down - 1)])
+    below = lax.ppermute(downward, "rows", [(i + 1, i) for i in range(down - 1)])
+
+    guarded = (frames + 2) * plan.stride
+    part, inner, kept = call(
+        functools.partial(first_kernel, plan),
         [
-            (pair, BF16),
-            (pair, BF16),
             ((2, cols * frames, 2 * chans), F32),
             ((max(groups - 1, 1), cols, frames, 6 * chans), BF16),
             ((rows, block, frames, chans), BF16),
@@ -328,24 +366,23 @@
         [
             ((groups, block + 4, frames, 6 * chans), BF16),
             ((groups, guarded, chans), F32),
-            ((groups, across * plan.unit, chans), F32),
+            ((groups, across * unit, chans), F32),
             ((cols, 2, frames + 8, chans), F32),
         ],
-        (own, gain1, conv_first, conv_second),
+        (*pieces, gain1, pw1),
         "first",
         pair_flops * 2 * groups,
         24 << 20,
     )
 
-    wqkv = jnp.concatenate([query_weight, key_weight, value_weight], axis=1)
     count = rows * block * frames
-    out = call(
-        second_kernel,
-        plan,
-        [((frames, rows, plan.wide_out, chans), BF16)],
+    outs = call(
+        functools.partial(second_kernel, plan),
+        [((2, few, rows, plan.wide_out, chans), BF16)] * chips,
         [
             ((2, block + 4, frames, 6 * chans), BF16),
             ((2, guarded, chans), F32),
+            ((2, across * unit, chans), F32),
             ((2, cols, frames, 6 * chans), BF16),
             ((2, cols, 2, frames + 8, chans), F32),
             ((count, chans), BF16),
@@ -358,15 +395,14 @@
         24 << 20,
     )
 
-    sent = out.reshape(across, few, rows, plan.wide_out, chans)
-    got = lax.all_to_all(sent, "tm", 0, 0, tiled=True)
-    length = round_up(max((across - 1) * block + plan.wide_out, width), 8)
+    gots = [outs[0]] + [exchange(outs[d], 2 * d) for d in range(1, chips)]
+    rec = exchange(jnp.stack([g[1] for g in gots]), 1)
+    length = round_up(max(across * block, width), 8)
     return call(
-        unpack_kernel,
-        plan,
+        functools.partial(unpack_kernel, plan),
         [((few, rows, width, chans), BF16)],
         [((few * rows, length, chans), F32)],
-        (got,),
+        (*gots, rec),
         "unpack",
         0,
         8 << 20,

time: 38.6 us -> 32.9 us (0.85)
  blocking collectives: 21.9 us -> 0 us
  starting transfers between devices: 4.78 us -> 14.4 us
  waiting for transfers between devices: 0.06 us -> 8.97 us
  local copies, waits for them, and re-layouts: 3.96 us -> 1 us
  Pallas kernels: 6.57 us -> 8.08 us
  other arithmetic: 0.81 us -> 0.07 us
    all_to_all x2 -> x0, blocking collectives: 21.9 us -> none  [the longest x1 12.6 us: local(): own = lax.all_to_all(sent, 'tm', 0, 0, tiled=True)]
    ppermute x2 -> x10, starting transfers between devices: 4.78 us -> 14.4 us  [the longest x8 8.57 us: exchange(): return lax.ppermute(value, 'tm', [(i, i ^ distance) for i in range(size)])]
    ppermute x2 -> x10, waiting for transfers between devices: 0.06 us -> 8.97 us  [the longest x8 8.11 us: exchange(): return lax.ppermute(value, 'tm', [(i, i ^ distance) for i in range(size)])]
    unnamed x12 -> x8, local copies, waits for them, and re-layouts: 3.94 us -> 0.96 us
    pallas_call x4 -> x6, Pallas kernels: 6.57 us -> 8.08 us  [call(): pl.pallas_call(kernel, out_shape=shapes[0] if single else shapes, in_spec...]
    concatenate x1 -> x2, other arithmetic: 0.81 us -> 0.05 us  [the longest x1 0.03 us: local(): downward = jnp.concatenate([p[0] for p in pieces])]
  transfers between devices with their start and end apart: 2 -> 10, of which waited for: 1 -> 8; matrix products, arithmetic and copies ran while one was open for 2% -> 0% of each run, Pallas kernels for 6% -> 12%
where the time goes in v3:
time: 32.9 us; the launch traced here: 32.7 us
  starting transfers between devices  14.4 us (44%)
  waiting for transfers between devices  8.97 us (27%)
  Pallas kernels  8.08 us (25%)
  local copies, waits for them, and re-layouts  1 us (3%)
    ppermute x8, starting transfers between devices, exchange(): return lax.ppermute(value, 'tm', [(i, i ^ distance) for i in range(size)])  8.57 us
    ppermute x8, waiting for transfers between devices, exchange(): return lax.ppermute(value, 'tm', [(i, i ^ distance) for i in range(size)])  8.11 us
    pallas_call x6, Pallas kernels, call(): pl.pallas_call(kernel, out_shape=shapes[0] if single else shapes, in_spec...  8.08 us
    ppermute x1, starting transfers between devices, local(): above = lax.ppermute(upward, 'rows', [(i, i + 1) for i in range(down - 1)])  4.56 us
    ppermute x1, starting transfers between devices, local(): lax.ppermute(downward, 'rows', [(i + 1, i) for i in range(down - 1)])  1.29 us
    unnamed x8, local copies, waits for them, and re-layouts  0.96 us
    ppermute x1, waiting for transfers between devices, local(): above = lax.ppermute(upward, 'rows', [(i, i + 1) for i in range(down - 1)])  0.85 us
  transfers between devices with their start and end apart: 10, of which 8 were waited for; matrix products, arithmetic and copies ran while one was open for 0% of the time, Pallas kernels for 12%

profile of v3, /device:TPU:0, one launch (start us, length us, event | category | flops | bytes accessed | tf_op | source)
XLA Modules:
  0.0 32.7 jit_solution(10658543404332730693)
XLA Ops:
  0.0 0.5 %collective-permute-start = (bf16[2,4,120,128]{3,2,1,0:T(8,128)(2,1)}, bf16[2,4,120,128]{3,2,1,0:T(8,128)(2,1)S(1)}, u32[]{:S(2)}, u32[]{:S(2)}) collective-permute-start(bf16[2,4,120,128]{3,2,1,0:T(8,128)(2,1)} %video_ref.1), channel_id=1, source_target_pairs={{0,4},{4,0},{8,12},{12,8},{16,20},{20,16},{24,28},{28,24},{1,5},{5... | collective-permute-start | bytes 737288 | tf_op jit(solution)/shard_map/ppermute | solution.py:295
  0.5 0.9 %copy-done = bf16[2,4,120,128]{3,2,1,0:T(8,128)(2,1)S(1)} copy-done((bf16[2,4,120,128]{3,2,1,0:T(8,128)(2,1)S(1)}, bf16[2,4,120,128]{3,2,1,0:T(8,128)(2,1)}, u32[]{:S(2)}) %copy-start) | copy-done | bytes 245784
  1.4 0.1 pack_own.1
  1.5 0.3 collective-permute-done.video_ref
  1.8 0.1 pack_other.1
  1.9 2.9 %collective-permute-start.1 = (bf16[2,2,80,128]{3,2,1,0:T(8,128)(2,1)S(1)}, bf16[2,2,80,128]{3,2,1,0:T(8,128)(2,1)S(1)}, u32[]{:S(2)}, u32[]{:S(2)}) collective-permute-start(bf16[2,2,80,128]{3,2,1,0:T(8,128)(2,1)S(1)} %get-tuple-element.35), channel_id=1, source_target_pairs={{0,8},{4,12},{8,0},{12,4},{16,24},{20,28},{24,16},{28,20},{1,9},{5... | collective-permute-start | bytes 245768 | tf_op jit(solution)/shard_map/ppermute | solution.py:295
  4.8 1.5 %collective-permute-start.2 = (bf16[2,2,80,128]{3,2,1,0:T(8,128)(2,1)S(1)}, bf16[2,2,80,128]{3,2,1,0:T(8,128)(2,1)S(1)}, u32[]{:S(2)}, u32[]{:S(2)}) collective-permute-start(bf16[2,2,80,128]{3,2,1,0:T(8,128)(2,1)S(1)} %get-tuple-element.36), channel_id=1, source_target_pairs={{0,16},{4,20},{8,24},{12,28},{16,0},{20,4},{24,8},{28,12},{1,17},{... | collective-permute-start | bytes 245768 | tf_op jit(solution)/shard_map/ppermute | solution.py:295
  6.4 1.8 %prep.1 = (bf16[3,2,768,256]{3,2,1,0:T(8,128)(2,1)S(1)}, bf16[3,2,768,256]{3,2,1,0:T(8,128)(2,1)S(1)}, bf16[128,384]{1,0:T(8,128)(2,1)S(1)}) custom-call(bf16[3,3,3,128,128]{4,3,2,1,0:T(8,128)(2,1)} %refs_0_.1, bf16[3,3,3,128,128]{4,3,2,1,0:T(8,128)(2,1)} %refs_1_.1, bf16[128,128]{1,0:T(8,128)(2,1)} %refs_2_.1, bf16[128,128]{1,0:T(8,128)(2,1)} %refs_3_.1, ...), custom_call_target="tpu_custom_call" | custom-call | tf_op jit(solution)/shard_map/prep/pallas_call | solution.py:280
  8.2 1.9 %collective-permute-done.2.refs_2_ = bf16[2,2,80,128]{3,2,1,0:T(8,128)(2,1)S(1)} collective-permute-done((bf16[2,2,80,128]{3,2,1,0:T(8,128)(2,1)S(1)}, bf16[2,2,80,128]{3,2,1,0:T(8,128)(2,1)S(1)}, u32[]{:S(2)}, u32[]{:S(2)}) %collective-permute-start.2) | collective-permute-done | bytes 81952 | tf_op jit(solution)/shard_map/ppermute | solution.py:295
  10.1 1.6 %collective-permute-done.3.refs_3_ = bf16[2,2,80,128]{3,2,1,0:T(8,128)(2,1)S(1)} collective-permute-done((bf16[2,2,80,128]{3,2,1,0:T(8,128)(2,1)S(1)}, bf16[2,2,80,128]{3,2,1,0:T(8,128)(2,1)S(1)}, u32[]{:S(2)}, u32[]{:S(2)}) %collective-permute-start.3) | collective-permute-done | bytes 81952 | tf_op jit(solution)/shard_map/ppermute | solution.py:295
  11.8 1.3 %collective-permute-start.5 = (bf16[8,80,128]{2,1,0:T(8,128)(2,1)S(1)}, bf16[8,80,128]{2,1,0:T(8,128)(2,1)S(1)}, u32[]{:S(2)}, u32[]{:S(2)}) collective-permute-start(bf16[8,80,128]{2,1,0:T(8,128)(2,1)S(1)} %pad_maximum_fusion.1), channel_id=1, source_target_pairs={{1,0},{2,1},{3,2},{5,4},{6,5},{7,6},{9,8},{10,9},{11,10},{13,12},{... | collective-permute-start | bytes 491528 | tf_op jit(solution)/shard_map/ppermute | solution.py:356
  13.1 4.6 %collective-permute-start.4 = (bf16[8,80,128]{2,1,0:T(8,128)(2,1)S(1)}, bf16[8,80,128]{2,1,0:T(8,128)(2,1)S(1)}, u32[]{:S(2)}, u32[]{:S(2)}) collective-permute-start(bf16[8,80,128]{2,1,0:T(8,128)(2,1)S(1)} %pad_maximum_fusion), channel_id=1, source_target_pairs={{0,1},{1,2},{2,3},{4,5},{5,6},{6,7},{8,9},{9,10},{10,11},{12,13},{... | collective-permute-start | bytes 491528 | tf_op jit(solution)/shard_map/ppermute | solution.py:355
  17.7 1.9 %first.1 = (f32[2,272,256]{2,1,0:T(8,128)S(1)}, bf16[1,17,16,768]{3,2,1,0:T(8,128)(2,1)S(1)}, bf16[4,15,16,128]{3,2,1,0:T(8,128)(2,1)S(1)}) custom-call(bf16[2,2,80,128]{3,2,1,0:T(8,128)(2,1)S(1)} %get-tuple-element.41.refs_0_, bf16[2,2,80,128]{3,2,1,0:T(8,128)(2,1)S(1)} %collective-permute-done.1.refs_1_, ...), custom_call_target="tpu_custom_call" | custom-call | flops 1283457024 | bytes 1220608 | tf_op jit(solution)/shard_map/first/pallas_call | solution.py:280
  19.6 0.9 %collective-permute-done.4.refs_0_ = bf16[8,80,128]{2,1,0:T(8,128)(2,1)S(1)} collective-permute-done((bf16[8,80,128]{2,1,0:T(8,128)(2,1)S(1)}, bf16[8,80,128]{2,1,0:T(8,128)(2,1)S(1)}, u32[]{:S(2)}, u32[]{:S(2)}) %collective-permute-start.4) | collective-permute-done | bytes 163872 | tf_op jit(solution)/shard_map/ppermute | solution.py:355
  20.5 3.4 %second.1 = (bf16[2,2,4,16,128]{4,3,2,1,0:T(8,128)(2,1)S(1)}, bf16[2,2,4,16,128]{4,3,2,1,0:T(8,128)(2,1)S(1)}, bf16[2,2,4,16,128]{4,3,2,1,0:T(8,128)(2,1)S(1)}, bf16[2,2,4,16,128]{4,3,2,1,0:T(8,128)(2,1)S(1)}) custom-call(bf16[8,80,128]{2,1,0:T(8,128)(2,1)S(1)} %collective-permute-done.4.refs_0_, bf16[8,80,128]{2,1,0:T(8,128)(2,1)S(1)} %collective-permute-done.5.refs_1_, ...), custom_call_target="tpu_custom_call" | custom-call | flops 1925185536 | bytes 262144 | tf_op jit(solution)/shard_map/second/pallas_call | solution.py:280
  23.9 0.6 %collective-permute-start.6 = (bf16[2,2,4,16,128]{4,3,2,1,0:T(8,128)(2,1)S(1)}, bf16[2,2,4,16,128]{4,3,2,1,0:T(8,128)(2,1)S(1)}, u32[]{:S(2)}, u32[]{:S(2)}) collective-permute-start(bf16[2,2,4,16,128]{4,3,2,1,0:T(8,128)(2,1)S(1)} %get-tuple-element.52), channel_id=1, source_target_pairs={{0,8},{4,12},{8,0},{12,4},{16,24},{20,28},{24,16},{28,20},{1,9},{5... | collective-permute-start | bytes 196616 | tf_op jit(solution)/shard_map/ppermute | solution.py:295
  24.5 0.8 %collective-permute-start.7 = (bf16[2,2,4,16,128]{4,3,2,1,0:T(8,128)(2,1)S(1)}, bf16[2,2,4,16,128]{4,3,2,1,0:T(8,128)(2,1)S(1)}, u32[]{:S(2)}, u32[]{:S(2)}) collective-permute-start(bf16[2,2,4,16,128]{4,3,2,1,0:T(8,128)(2,1)S(1)} %get-tuple-element.53), channel_id=1, source_target_pairs={{0,16},{4,20},{8,24},{12,28},{16,0},{20,4},{24,8},{28,12},{1,17},{... | collective-permute-start | bytes 196616 | tf_op jit(solution)/shard_map/ppermute | solution.py:295
  25.3 2.2 %collective-permute-start.8 = (bf16[2,2,4,16,128]{4,3,2,1,0:T(8,128)(2,1)S(1)}, bf16[2,2,4,16,128]{4,3,2,1,0:T(8,128)(2,1)S(1)}, u32[]{:S(2)}, u32[]{:S(2)}) collective-permute-start(bf16[2,2,4,16,128]{4,3,2,1,0:T(8,128)(2,1)S(1)} %get-tuple-element.54), channel_id=1, source_target_pairs={{0,24},{4,28},{8,16},{12,20},{16,8},{20,12},{24,0},{28,4},{1,25},{... | collective-permute-start | bytes 196616 | tf_op jit(solution)/shard_map/ppermute | solution.py:295
  27.4 0.8 %collective-permute-done.6.refs_1_ = bf16[2,2,4,16,128]{4,3,2,1,0:T(8,128)(2,1)S(1)} collective-permute-done((bf16[2,2,4,16,128]{4,3,2,1,0:T(8,128)(2,1)S(1)}, bf16[2,2,4,16,128]{4,3,2,1,0:T(8,128)(2,1)S(1)}, u32[]{:S(2)}, u32[]{:S(2)}) %collective-permute-start.6) | collective-permute-done | bytes 65568 | tf_op jit(solution)/shard_map/ppermute | solution.py:295
  28.2 0.5 %collective-permute-done.7.refs_2_ = bf16[2,2,4,16,128]{4,3,2,1,0:T(8,128)(2,1)S(1)} collective-permute-done((bf16[2,2,4,16,128]{4,3,2,1,0:T(8,128)(2,1)S(1)}, bf16[2,2,4,16,128]{4,3,2,1,0:T(8,128)(2,1)S(1)}, u32[]{:S(2)}, u32[]{:S(2)}) %collective-permute-start.7) | collective-permute-done | bytes 65568 | tf_op jit(solution)/shard_map/ppermute | solution.py:295
  28.8 1.7 %collective-permute-done.8.refs_3_ = bf16[2,2,4,16,128]{4,3,2,1,0:T(8,128)(2,1)S(1)} collective-permute-done((bf16[2,2,4,16,128]{4,3,2,1,0:T(8,128)(2,1)S(1)}, bf16[2,2,4,16,128]{4,3,2,1,0:T(8,128)(2,1)S(1)}, u32[]{:S(2)}, u32[]{:S(2)}) %collective-permute-start.8) | collective-permute-done | bytes 65568 | tf_op jit(solution)/shard_map/ppermute | solution.py:295
  30.5 0.1 collective-permute-start.9
  30.5 1.3 %collective-permute-done.9.refs_4_ = bf16[4,2,4,16,128]{4,3,2,1,0:T(8,128)(2,1)S(1)} collective-permute-done((bf16[4,2,4,16,128]{4,3,2,1,0:T(8,128)(2,1)S(1)}, bf16[4,2,4,16,128]{4,3,2,1,0:T(8,128)(2,1)S(1)}, u32[]{:S(2)}, u32[]{:S(2)}) %collective-permute-start.9) | collective-permute-done | bytes 131104 | tf_op jit(solution)/shard_map/ppermute | solution.py:295
  31.9 0.8 %unpack.1 = bf16[2,4,120,128]{3,2,1,0:T(8,128)(2,1)} custom-call(bf16[2,2,4,16,128]{4,3,2,1,0:T(8,128)(2,1)S(1)} %get-tuple-element.51.refs_0_, bf16[2,2,4,16,128]{4,3,2,1,0:T(8,128)(2,1)S(1)} %collective-permute-done.6.refs_1_, bf16[2,2,4,16,128]{4,3,2,1,0:T(8,128)(2,1)S(1)} %collective-permute-done.7.refs_2_, ...), custom_call_target="tpu_custom_call" | custom-call | tf_op jit(solution)/shard_map/unpack/pallas_call | solution.py:280
  (19 shorter events, 0.2 us)
Async XLA Ops:
  0.0 1.8 %collective-permute-start = (bf16[2,4,120,128]{3,2,1,0:T(8,128)(2,1)}, bf16[2,4,120,128]{3,2,1,0:T(8,128)(2,1)S(1)}, u32[]{:S(2)}, u32[]{:S(2)}) collective-permute-start(bf16[2,4,120,128]{3,2,1,0:T(8,128)(2,1)} %video_ref.1), channel_id=1, source_target_pairs={{0,4},{4,0},{8,12},{12,8},{16,20},{20,16},{24,28},{28,24},{1,5},{5... | collective-permute-start | bytes 737288 | tf_op jit(solution)/shard_map/ppermute | solution.py:295
  0.5 0.9 %copy-start = (bf16[2,4,120,128]{3,2,1,0:T(8,128)(2,1)S(1)}, bf16[2,4,120,128]{3,2,1,0:T(8,128)(2,1)}, u32[]{:S(2)}) copy-start(bf16[2,4,120,128]{3,2,1,0:T(8,128)(2,1)} %video_ref.1) | copy-start | bytes 737284
  1.4 16.2 %copy-start.2 = (bf16[128]{0:T(256)(128)(2,1)S(1)}, bf16[128]{0:T(256)(128)(2,1)}, u32[]{:S(2)}) copy-start(bf16[128]{0:T(256)(128)(2,1)} %param.10) | copy-start | bytes 772
  1.9 6.3 %collective-permute-start.1 = (bf16[2,2,80,128]{3,2,1,0:T(8,128)(2,1)S(1)}, bf16[2,2,80,128]{3,2,1,0:T(8,128)(2,1)S(1)}, u32[]{:S(2)}, u32[]{:S(2)}) collective-permute-start(bf16[2,2,80,128]{3,2,1,0:T(8,128)(2,1)S(1)} %get-tuple-element.35), channel_id=1, source_target_pairs={{0,8},{4,12},{8,0},{12,4},{16,24},{20,28},{24,16},{28,20},{1,9},{5... | collective-permute-start | bytes 245768 | tf_op jit(solution)/shard_map/ppermute | solution.py:295
  4.8 5.3 %collective-permute-start.2 = (bf16[2,2,80,128]{3,2,1,0:T(8,128)(2,1)S(1)}, bf16[2,2,80,128]{3,2,1,0:T(8,128)(2,1)S(1)}, u32[]{:S(2)}, u32[]{:S(2)}) collective-permute-start(bf16[2,2,80,128]{3,2,1,0:T(8,128)(2,1)S(1)} %get-tuple-element.36), channel_id=1, source_target_pairs={{0,16},{4,20},{8,24},{12,28},{16,0},{20,4},{24,8},{28,12},{1,17},{... | collective-permute-start | bytes 245768 | tf_op jit(solution)/shard_map/ppermute | solution.py:295
  6.4 5.3 %collective-permute-start.3 = (bf16[2,2,80,128]{3,2,1,0:T(8,128)(2,1)S(1)}, bf16[2,2,80,128]{3,2,1,0:T(8,128)(2,1)S(1)}, u32[]{:S(2)}, u32[]{:S(2)}) collective-permute-start(bf16[2,2,80,128]{3,2,1,0:T(8,128)(2,1)S(1)} %get-tuple-element.37), channel_id=1, source_target_pairs={{0,24},{4,28},{8,16},{12,20},{16,8},{20,12},{24,0},{28,4},{1,25},{... | collective-permute-start | bytes 245768 | tf_op jit(solution)/shard_map/ppermute | solution.py:295
  11.8 7.8 %collective-permute-start.5 = (bf16[8,80,128]{2,1,0:T(8,128)(2,1)S(1)}, bf16[8,80,128]{2,1,0:T(8,128)(2,1)S(1)}, u32[]{:S(2)}, u32[]{:S(2)}) collective-permute-start(bf16[8,80,128]{2,1,0:T(8,128)(2,1)S(1)} %pad_maximum_fusion.1), channel_id=1, source_target_pairs={{1,0},{2,1},{3,2},{5,4},{6,5},{7,6},{9,8},{10,9},{11,10},{13,12},{... | collective-permute-start | bytes 491528 | tf_op jit(solution)/shard_map/ppermute | solution.py:356
  13.1 7.4 %collective-permute-start.4 = (bf16[8,80,128]{2,1,0:T(8,128)(2,1)S(1)}, bf16[8,80,128]{2,1,0:T(8,128)(2,1)S(1)}, u32[]{:S(2)}, u32[]{:S(2)}) collective-permute-start(bf16[8,80,128]{2,1,0:T(8,128)(2,1)S(1)} %pad_maximum_fusion), channel_id=1, source_target_pairs={{0,1},{1,2},{2,3},{4,5},{5,6},{6,7},{8,9},{9,10},{10,11},{12,13},{... | collective-permute-start | bytes 491528 | tf_op jit(solution)/shard_map/ppermute | solution.py:355
  17.7 2.8 %copy-start.1 = (bf16[128,128]{1,0:T(8,128)(2,1)S(1)}, bf16[128,128]{1,0:T(8,128)(2,1)}, u32[]{:S(2)}) copy-start(bf16[128,128]{1,0:T(8,128)(2,1)} %refs_10_.1) | copy-start | bytes 98308
  17.7 2.8 %copy-start.3 = (bf16[128]{0:T(256)(128)(2,1)S(1)}, bf16[128]{0:T(256)(128)(2,1)}, u32[]{:S(2)}) copy-start(bf16[128]{0:T(256)(128)(2,1)} %param.13) | copy-start | bytes 772
  23.9 4.3 %collective-permute-start.6 = (bf16[2,2,4,16,128]{4,3,2,1,0:T(8,128)(2,1)S(1)}, bf16[2,2,4,16,128]{4,3,2,1,0:T(8,128)(2,1)S(1)}, u32[]{:S(2)}, u32[]{:S(2)}) collective-permute-start(bf16[2,2,4,16,128]{4,3,2,1,0:T(8,128)(2,1)S(1)} %get-tuple-element.52), channel_id=1, source_target_pairs={{0,8},{4,12},{8,0},{12,4},{16,24},{20,28},{24,16},{28,20},{1,9},{5... | collective-permute-start | bytes 196616 | tf_op jit(solution)/shard_map/ppermute | solution.py:295
  24.5 4.3 %collective-permute-start.7 = (bf16[2,2,4,16,128]{4,3,2,1,0:T(8,128)(2,1)S(1)}, bf16[2,2,4,16,128]{4,3,2,1,0:T(8,128)(2,1)S(1)}, u32[]{:S(2)}, u32[]{:S(2)}) collective-permute-start(bf16[2,2,4,16,128]{4,3,2,1,0:T(8,128)(2,1)S(1)} %get-tuple-element.53), channel_id=1, source_target_pairs={{0,16},{4,20},{8,24},{12,28},{16,0},{20,4},{24,8},{28,12},{1,17},{... | collective-permute-start | bytes 196616 | tf_op jit(solution)/shard_map/ppermute | solution.py:295
  25.3 5.2 %collective-permute-start.8 = (bf16[2,2,4,16,128]{4,3,2,1,0:T(8,128)(2,1)S(1)}, bf16[2,2,4,16,128]{4,3,2,1,0:T(8,128)(2,1)S(1)}, u32[]{:S(2)}, u32[]{:S(2)}) collective-permute-start(bf16[2,2,4,16,128]{4,3,2,1,0:T(8,128)(2,1)S(1)} %get-tuple-element.54), channel_id=1, source_target_pairs={{0,24},{4,28},{8,16},{12,20},{16,8},{20,12},{24,0},{28,4},{1,25},{... | collective-permute-start | bytes 196616 | tf_op jit(solution)/shard_map/ppermute | solution.py:295
  30.5 1.4 %collective-permute-start.9 = (bf16[4,2,4,16,128]{4,3,2,1,0:T(8,128)(2,1)S(1)}, bf16[4,2,4,16,128]{4,3,2,1,0:T(8,128)(2,1)S(1)}, u32[]{:S(2)}, u32[]{:S(2)}) collective-permute-start(bf16[4,2,4,16,128]{4,3,2,1,0:T(8,128)(2,1)S(1)} %pad_maximum_fusion.2), channel_id=1, source_target_pairs={{0,4},{4,0},{8,12},{12,8},{16,20},{20,16},{24,28},{28,24},{1,5},{5... | collective-permute-start | bytes 393224 | tf_op jit(solution)/shard_map/ppermute | solution.py:295

commit v4 on v3

--- a/solution.py
+++ b/solution.py
@@ -190,7 +190,7 @@
 
 
 def second_kernel(plan, *refs):
-    sides, refs = refs[:2], refs[2:]
+    swaps, refs = refs[:2], refs[2:]
     gain1_ref, pw1, pw2, part_ref, mid_ref, kept_ref, gain2_ref, wqkv_ref, wo_ref = refs[:9]
     outs, refs = refs[9 : 9 + plan.chips], refs[9 + plan.chips :]
     taps, act, raw, mid, hold, hid, qkv, back = refs
@@ -199,8 +199,11 @@
     gain2 = gain2_ref[...].astype(F32)
 
     totals = []
-    for side, ref in enumerate(sides):
+    odd = lax.rem(lax.axis_index("rows"), 2)
+    for order, ref in enumerate(swaps):
+        side = odd if order == 0 else 1 - odd
         in_order(plan, lambda i: ref[i], raw.at[side])
+    for side in range(2):
         act_taps(plan, raw[side], gain1, act.at[side], taps, side)
     for side in range(2):
         total = half_conv(plan, [(taps, side, 1)], pw1, side, plan.cols)
@@ -350,10 +353,15 @@
     )
     pieces, (pw1, pw2, wqkv) = lax.optimization_barrier((pieces, prepared))
 
+    even = lax.axis_index("rows") % 2 == 0
     upward = jnp.concatenate([p[groups - 1] for p in pieces])
     downward = jnp.concatenate([p[0] for p in pieces])
-    above = lax.ppermute(upward, "rows", [(i, i + 1) for i in range(down - 1)])
-    below = lax.ppermute(downward, "rows", [(i + 1, i) for i in range(down - 1)])
+    swaps = []
+    for offset in (1, 0):
+        pairs = [(i, i + 1) for i in range(offset, down - 1, 2)]
+        pairs = pairs + [(j, i) for i, j in pairs]
+        ahead = even if offset == 0 else jnp.logical_not(even)
+        swaps.append(lax.ppermute(jnp.where(ahead, upward, downward), "rows", pairs))
 
     guarded = (frames + 2) * plan.stride
     part, inner, kept = call(
@@ -389,7 +397,7 @@
             ((count, 3 * chans), BF16),
             ((rows, frames * plan.wide_out, chans), F32),
         ],
-        (above, below, gain1, pw1, pw2, part, inner, kept, gain2, wqkv, out_weight),
+        (*swaps, gain1, pw1, pw2, part, inner, kept, gain2, wqkv, out_weight),
         "second",
         pair_flops * 2 * (groups + 1),
         24 << 20,

time: 32.9 us -> 32 us (0.973)
  the two profiles are of different devices: /device:TPU:0 before, /device:TPU:19 now
where the time goes in v4:
time: 32 us; the launch traced here: 31.8 us
  starting transfers between devices  14.9 us (47%)
  Pallas kernels  8.13 us (25%)
  waiting for transfers between devices  7.55 us (24%)
  local copies, waits for them, and re-layouts  1 us (3%)
    ppermute x8, starting transfers between devices, exchange(): return lax.ppermute(value, 'tm', [(i, i ^ distance) for i in range(size)])  11.6 us
    pallas_call x6, Pallas kernels, call(): pl.pallas_call(kernel, out_shape=shapes[0] if single else shapes, in_spec...  8.13 us
    ppermute x8, waiting for transfers between devices, exchange(): return lax.ppermute(value, 'tm', [(i, i ^ distance) for i in range(size)])  5.38 us
    ppermute x2, starting transfers between devices, local(): lax.ppermute(jnp.where(ahead, upward, downward), 'rows', pairs)  3.27 us
    ppermute x2, waiting for transfers between devices, local(): lax.ppermute(jnp.where(ahead, upward, downward), 'rows', pairs)  2.17 us
    unnamed x8, local copies, waits for them, and re-layouts  0.96 us
  transfers between devices with their start and end apart: 10, of which 7 were waited for; matrix products, arithmetic and copies ran while one was open for 0% of the time, Pallas kernels for 12%

profile of v4, /device:TPU:19, one launch (start us, length us, event | category | flops | bytes accessed | tf_op | source)
XLA Modules:
  0.0 31.8 jit_solution(5028779965096925933)
XLA Ops:
  0.0 0.7 %collective-permute-start = (bf16[2,4,120,128]{3,2,1,0:T(8,128)(2,1)}, bf16[2,4,120,128]{3,2,1,0:T(8,128)(2,1)S(1)}, u32[]{:S(2)}, u32[]{:S(2)}) collective-permute-start(bf16[2,4,120,128]{3,2,1,0:T(8,128)(2,1)} %video_ref.1), channel_id=1, source_target_pairs={{0,4},{4,0},{8,12},{12,8},{16,20},{20,16},{24,28},{28,24},{1,5},{5... | collective-permute-start | bytes 737288 | tf_op jit(solution)/shard_map/ppermute | solution.py:298
  0.7 0.9 %copy-done = bf16[2,4,120,128]{3,2,1,0:T(8,128)(2,1)S(1)} copy-done((bf16[2,4,120,128]{3,2,1,0:T(8,128)(2,1)S(1)}, bf16[2,4,120,128]{3,2,1,0:T(8,128)(2,1)}, u32[]{:S(2)}) %copy-start) | copy-done | bytes 245784
  1.6 0.1 pack_own.1
  1.7 0.3 collective-permute-done.video_ref
  2.0 0.1 pack_other.1
  2.1 0.3 %collective-permute-start.1 = (bf16[2,2,80,128]{3,2,1,0:T(8,128)(2,1)S(1)}, bf16[2,2,80,128]{3,2,1,0:T(8,128)(2,1)S(1)}, u32[]{:S(2)}, u32[]{:S(2)}) collective-permute-start(bf16[2,2,80,128]{3,2,1,0:T(8,128)(2,1)S(1)} %get-tuple-element.35), channel_id=1, source_target_pairs={{0,8},{4,12},{8,0},{12,4},{16,24},{20,28},{24,16},{28,20},{1,9},{5... | collective-permute-start | bytes 245768 | tf_op jit(solution)/shard_map/ppermute | solution.py:298
  2.4 1.2 %collective-permute-start.2 = (bf16[2,2,80,128]{3,2,1,0:T(8,128)(2,1)S(1)}, bf16[2,2,80,128]{3,2,1,0:T(8,128)(2,1)S(1)}, u32[]{:S(2)}, u32[]{:S(2)}) collective-permute-start(bf16[2,2,80,128]{3,2,1,0:T(8,128)(2,1)S(1)} %get-tuple-element.36), channel_id=1, source_target_pairs={{0,16},{4,20},{8,24},{12,28},{16,0},{20,4},{24,8},{28,12},{1,17},{... | collective-permute-start | bytes 245768 | tf_op jit(solution)/shard_map/ppermute | solution.py:298
  3.7 1.2 %collective-permute-start.3 = (bf16[2,2,80,128]{3,2,1,0:T(8,128)(2,1)S(1)}, bf16[2,2,80,128]{3,2,1,0:T(8,128)(2,1)S(1)}, u32[]{:S(2)}, u32[]{:S(2)}) collective-permute-start(bf16[2,2,80,128]{3,2,1,0:T(8,128)(2,1)S(1)} %get-tuple-element.37), channel_id=1, source_target_pairs={{0,24},{4,28},{8,16},{12,20},{16,8},{20,12},{24,0},{28,4},{1,25},{... | collective-permute-start | bytes 245768 | tf_op jit(solution)/shard_map/ppermute | solution.py:298
  4.8 1.8 %prep.1 = (bf16[3,2,768,256]{3,2,1,0:T(8,128)(2,1)S(1)}, bf16[3,2,768,256]{3,2,1,0:T(8,128)(2,1)S(1)}, bf16[128,384]{1,0:T(8,128)(2,1)S(1)}) custom-call(bf16[3,3,3,128,128]{4,3,2,1,0:T(8,128)(2,1)} %refs_0_.1, bf16[3,3,3,128,128]{4,3,2,1,0:T(8,128)(2,1)} %refs_1_.1, bf16[128,128]{1,0:T(8,128)(2,1)} %refs_2_.1, bf16[128,128]{1,0:T(8,128)(2,1)} %refs_3_.1, ...), custom_call_target="tpu_custom_call" | custom-call | tf_op jit(solution)/shard_map/prep/pallas_call | solution.py:283
  6.7 1.5 %collective-permute-done.3.refs_3_ = bf16[2,2,80,128]{3,2,1,0:T(8,128)(2,1)S(1)} collective-permute-done((bf16[2,2,80,128]{3,2,1,0:T(8,128)(2,1)S(1)}, bf16[2,2,80,128]{3,2,1,0:T(8,128)(2,1)S(1)}, u32[]{:S(2)}, u32[]{:S(2)}) %collective-permute-start.3) | collective-permute-done | bytes 81952 | tf_op jit(solution)/shard_map/ppermute | solution.py:298
  8.3 1.4 %collective-permute-start.5 = (bf16[8,80,128]{2,1,0:T(8,128)(2,1)S(1)}, bf16[8,80,128]{2,1,0:T(8,128)(2,1)S(1)}, u32[]{:S(2)}, u32[]{:S(2)}) collective-permute-start(bf16[8,80,128]{2,1,0:T(8,128)(2,1)S(1)} %get-tuple-element.55), channel_id=1, source_target_pairs={{0,1},{2,3},{1,0},{3,2},{4,5},{6,7},{5,4},{7,6},{8,9},{10,11},{9,8... | collective-permute-start | bytes 491528 | tf_op jit(solution)/shard_map/ppermute | solution.py:364
  9.6 1.9 %collective-permute-start.4 = (bf16[8,80,128]{2,1,0:T(8,128)(2,1)S(1)}, bf16[8,80,128]{2,1,0:T(8,128)(2,1)S(1)}, u32[]{:S(2)}, u32[]{:S(2)}) collective-permute-start(bf16[8,80,128]{2,1,0:T(8,128)(2,1)S(1)} %get-tuple-element.56), channel_id=1, source_target_pairs={{1,2},{2,1},{5,6},{6,5},{9,10},{10,9},{13,14},{14,13},{17,18},{18,... | collective-permute-start | bytes 491528 | tf_op jit(solution)/shard_map/ppermute | solution.py:364
  11.6 1.9 %first.1 = (f32[2,272,256]{2,1,0:T(8,128)S(1)}, bf16[1,17,16,768]{3,2,1,0:T(8,128)(2,1)S(1)}, bf16[4,15,16,128]{3,2,1,0:T(8,128)(2,1)S(1)}) custom-call(bf16[2,2,80,128]{3,2,1,0:T(8,128)(2,1)S(1)} %get-tuple-element.41.refs_0_, bf16[2,2,80,128]{3,2,1,0:T(8,128)(2,1)S(1)} %collective-permute-done.1.refs_1_, ...), custom_call_target="tpu_custom_call" | custom-call | flops 1283457024 | bytes 1220608 | tf_op jit(solution)/shard_map/first/pallas_call | solution.py:283
  13.5 2.2 %collective-permute-done.4.refs_0_ = bf16[8,80,128]{2,1,0:T(8,128)(2,1)S(1)} collective-permute-done((bf16[8,80,128]{2,1,0:T(8,128)(2,1)S(1)}, bf16[8,80,128]{2,1,0:T(8,128)(2,1)S(1)}, u32[]{:S(2)}, u32[]{:S(2)}) %collective-permute-start.4) | collective-permute-done | bytes 163872 | tf_op jit(solution)/shard_map/ppermute | solution.py:364
  15.7 3.4 %second.1 = (bf16[2,2,4,16,128]{4,3,2,1,0:T(8,128)(2,1)S(1)}, bf16[2,2,4,16,128]{4,3,2,1,0:T(8,128)(2,1)S(1)}, bf16[2,2,4,16,128]{4,3,2,1,0:T(8,128)(2,1)S(1)}, bf16[2,2,4,16,128]{4,3,2,1,0:T(8,128)(2,1)S(1)}) custom-call(bf16[8,80,128]{2,1,0:T(8,128)(2,1)S(1)} %collective-permute-done.4.refs_0_, bf16[8,80,128]{2,1,0:T(8,128)(2,1)S(1)} %collective-permute-done.5.refs_1_, ...), custom_call_target="tpu_custom_call" | custom-call | flops 1925185536 | bytes 262144 | tf_op jit(solution)/shard_map/second/pallas_call | solution.py:283
  19.1 1.0 %collective-permute-start.6 = (bf16[2,2,4,16,128]{4,3,2,1,0:T(8,128)(2,1)S(1)}, bf16[2,2,4,16,128]{4,3,2,1,0:T(8,128)(2,1)S(1)}, u32[]{:S(2)}, u32[]{:S(2)}) collective-permute-start(bf16[2,2,4,16,128]{4,3,2,1,0:T(8,128)(2,1)S(1)} %get-tuple-element.52), channel_id=1, source_target_pairs={{0,8},{4,12},{8,0},{12,4},{16,24},{20,28},{24,16},{28,20},{1,9},{5... | collective-permute-start | bytes 196616 | tf_op jit(solution)/shard_map/ppermute | solution.py:298
  20.1 0.3 %collective-permute-start.7 = (bf16[2,2,4,16,128]{4,3,2,1,0:T(8,128)(2,1)S(1)}, bf16[2,2,4,16,128]{4,3,2,1,0:T(8,128)(2,1)S(1)}, u32[]{:S(2)}, u32[]{:S(2)}) collective-permute-start(bf16[2,2,4,16,128]{4,3,2,1,0:T(8,128)(2,1)S(1)} %get-tuple-element.53), channel_id=1, source_target_pairs={{0,16},{4,20},{8,24},{12,28},{16,0},{20,4},{24,8},{28,12},{1,17},{... | collective-permute-start | bytes 196616 | tf_op jit(solution)/shard_map/ppermute | solution.py:298
  20.4 1.4 %collective-permute-start.8 = (bf16[2,2,4,16,128]{4,3,2,1,0:T(8,128)(2,1)S(1)}, bf16[2,2,4,16,128]{4,3,2,1,0:T(8,128)(2,1)S(1)}, u32[]{:S(2)}, u32[]{:S(2)}) collective-permute-start(bf16[2,2,4,16,128]{4,3,2,1,0:T(8,128)(2,1)S(1)} %get-tuple-element.54), channel_id=1, source_target_pairs={{0,24},{4,28},{8,16},{12,20},{16,8},{20,12},{24,0},{28,4},{1,25},{... | collective-permute-start | bytes 196616 | tf_op jit(solution)/shard_map/ppermute | solution.py:298
  21.9 0.5 %collective-permute-done.6.refs_1_ = bf16[2,2,4,16,128]{4,3,2,1,0:T(8,128)(2,1)S(1)} collective-permute-done((bf16[2,2,4,16,128]{4,3,2,1,0:T(8,128)(2,1)S(1)}, bf16[2,2,4,16,128]{4,3,2,1,0:T(8,128)(2,1)S(1)}, u32[]{:S(2)}, u32[]{:S(2)}) %collective-permute-start.6) | collective-permute-done | bytes 65568 | tf_op jit(solution)/shard_map/ppermute | solution.py:298
  22.3 0.9 %collective-permute-done.7.refs_2_ = bf16[2,2,4,16,128]{4,3,2,1,0:T(8,128)(2,1)S(1)} collective-permute-done((bf16[2,2,4,16,128]{4,3,2,1,0:T(8,128)(2,1)S(1)}, bf16[2,2,4,16,128]{4,3,2,1,0:T(8,128)(2,1)S(1)}, u32[]{:S(2)}, u32[]{:S(2)}) %collective-permute-start.7) | collective-permute-done | bytes 65568 | tf_op jit(solution)/shard_map/ppermute | solution.py:298
  23.2 1.2 %collective-permute-done.8.refs_3_ = bf16[2,2,4,16,128]{4,3,2,1,0:T(8,128)(2,1)S(1)} collective-permute-done((bf16[2,2,4,16,128]{4,3,2,1,0:T(8,128)(2,1)S(1)}, bf16[2,2,4,16,128]{4,3,2,1,0:T(8,128)(2,1)S(1)}, u32[]{:S(2)}, u32[]{:S(2)}) %collective-permute-start.8) | collective-permute-done | bytes 65568 | tf_op jit(solution)/shard_map/ppermute | solution.py:298
  24.5 5.5 %collective-permute-start.9 = (bf16[4,2,4,16,128]{4,3,2,1,0:T(8,128)(2,1)S(1)}, bf16[4,2,4,16,128]{4,3,2,1,0:T(8,128)(2,1)S(1)}, u32[]{:S(2)}, u32[]{:S(2)}) collective-permute-start(bf16[4,2,4,16,128]{4,3,2,1,0:T(8,128)(2,1)S(1)} %pad_maximum_fusion.2), channel_id=1, source_target_pairs={{0,4},{4,0},{8,12},{12,8},{16,20},{20,16},{24,28},{28,24},{1,5},{5... | collective-permute-start | bytes 393224 | tf_op jit(solution)/shard_map/ppermute | solution.py:298
  30.0 1.0 %collective-permute-done.9.refs_4_ = bf16[4,2,4,16,128]{4,3,2,1,0:T(8,128)(2,1)S(1)} collective-permute-done((bf16[4,2,4,16,128]{4,3,2,1,0:T(8,128)(2,1)S(1)}, bf16[4,2,4,16,128]{4,3,2,1,0:T(8,128)(2,1)S(1)}, u32[]{:S(2)}, u32[]{:S(2)}) %collective-permute-start.9) | collective-permute-done | bytes 131104 | tf_op jit(solution)/shard_map/ppermute | solution.py:298
  31.0 0.8 %unpack.1 = bf16[2,4,120,128]{3,2,1,0:T(8,128)(2,1)} custom-call(bf16[2,2,4,16,128]{4,3,2,1,0:T(8,128)(2,1)S(1)} %get-tuple-element.51.refs_0_, bf16[2,2,4,16,128]{4,3,2,1,0:T(8,128)(2,1)S(1)} %collective-permute-done.6.refs_1_, bf16[2,2,4,16,128]{4,3,2,1,0:T(8,128)(2,1)S(1)} %collective-permute-done.7.refs_2_, ...), custom_call_target="tpu_custom_call" | custom-call | tf_op jit(solution)/shard_map/unpack/pallas_call | solution.py:283
  (18 shorter events, 0.1 us)
Async XLA Ops:
  0.0 2.0 %collective-permute-start = (bf16[2,4,120,128]{3,2,1,0:T(8,128)(2,1)}, bf16[2,4,120,128]{3,2,1,0:T(8,128)(2,1)S(1)}, u32[]{:S(2)}, u32[]{:S(2)}) collective-permute-start(bf16[2,4,120,128]{3,2,1,0:T(8,128)(2,1)} %video_ref.1), channel_id=1, source_target_pairs={{0,4},{4,0},{8,12},{12,8},{16,20},{20,16},{24,28},{28,24},{1,5},{5... | collective-permute-start | bytes 737288 | tf_op jit(solution)/shard_map/ppermute | solution.py:298
  0.7 0.9 %copy-start = (bf16[2,4,120,128]{3,2,1,0:T(8,128)(2,1)S(1)}, bf16[2,4,120,128]{3,2,1,0:T(8,128)(2,1)}, u32[]{:S(2)}) copy-start(bf16[2,4,120,128]{3,2,1,0:T(8,128)(2,1)} %video_ref.1) | copy-start | bytes 737284
  1.6 9.9 %copy-start.2 = (bf16[128]{0:T(256)(128)(2,1)S(1)}, bf16[128]{0:T(256)(128)(2,1)}, u32[]{:S(2)}) copy-start(bf16[128]{0:T(256)(128)(2,1)} %param.10) | copy-start | bytes 772
  2.1 4.5 %collective-permute-start.1 = (bf16[2,2,80,128]{3,2,1,0:T(8,128)(2,1)S(1)}, bf16[2,2,80,128]{3,2,1,0:T(8,128)(2,1)S(1)}, u32[]{:S(2)}, u32[]{:S(2)}) collective-permute-start(bf16[2,2,80,128]{3,2,1,0:T(8,128)(2,1)S(1)} %get-tuple-element.35), channel_id=1, source_target_pairs={{0,8},{4,12},{8,0},{12,4},{16,24},{20,28},{24,16},{28,20},{1,9},{5... | collective-permute-start | bytes 245768 | tf_op jit(solution)/shard_map/ppermute | solution.py:298
  2.4 4.2 %collective-permute-start.2 = (bf16[2,2,80,128]{3,2,1,0:T(8,128)(2,1)S(1)}, bf16[2,2,80,128]{3,2,1,0:T(8,128)(2,1)S(1)}, u32[]{:S(2)}, u32[]{:S(2)}) collective-permute-start(bf16[2,2,80,128]{3,2,1,0:T(8,128)(2,1)S(1)} %get-tuple-element.36), channel_id=1, source_target_pairs={{0,16},{4,20},{8,24},{12,28},{16,0},{20,4},{24,8},{28,12},{1,17},{... | collective-permute-start | bytes 245768 | tf_op jit(solution)/shard_map/ppermute | solution.py:298
  3.7 4.5 %collective-permute-start.3 = (bf16[2,2,80,128]{3,2,1,0:T(8,128)(2,1)S(1)}, bf16[2,2,80,128]{3,2,1,0:T(8,128)(2,1)S(1)}, u32[]{:S(2)}, u32[]{:S(2)}) collective-permute-start(bf16[2,2,80,128]{3,2,1,0:T(8,128)(2,1)S(1)} %get-tuple-element.37), channel_id=1, source_target_pairs={{0,24},{4,28},{8,16},{12,20},{16,8},{20,12},{24,0},{28,4},{1,25},{... | collective-permute-start | bytes 245768 | tf_op jit(solution)/shard_map/ppermute | solution.py:298
  8.3 5.2 %collective-permute-start.5 = (bf16[8,80,128]{2,1,0:T(8,128)(2,1)S(1)}, bf16[8,80,128]{2,1,0:T(8,128)(2,1)S(1)}, u32[]{:S(2)}, u32[]{:S(2)}) collective-permute-start(bf16[8,80,128]{2,1,0:T(8,128)(2,1)S(1)} %get-tuple-element.55), channel_id=1, source_target_pairs={{0,1},{2,3},{1,0},{3,2},{4,5},{6,7},{5,4},{7,6},{8,9},{10,11},{9,8... | collective-permute-start | bytes 491528 | tf_op jit(solution)/shard_map/ppermute | solution.py:364
  9.6 6.1 %collective-permute-start.4 = (bf16[8,80,128]{2,1,0:T(8,128)(2,1)S(1)}, bf16[8,80,128]{2,1,0:T(8,128)(2,1)S(1)}, u32[]{:S(2)}, u32[]{:S(2)}) collective-permute-start(bf16[8,80,128]{2,1,0:T(8,128)(2,1)S(1)} %get-tuple-element.56), channel_id=1, source_target_pairs={{1,2},{2,1},{5,6},{6,5},{9,10},{10,9},{13,14},{14,13},{17,18},{18,... | collective-permute-start | bytes 491528 | tf_op jit(solution)/shard_map/ppermute | solution.py:364
  11.6 4.1 %copy-start.1 = (bf16[128,128]{1,0:T(8,128)(2,1)S(1)}, bf16[128,128]{1,0:T(8,128)(2,1)}, u32[]{:S(2)}) copy-start(bf16[128,128]{1,0:T(8,128)(2,1)} %refs_10_.1) | copy-start | bytes 98308
  11.6 4.1 %copy-start.3 = (bf16[128]{0:T(256)(128)(2,1)S(1)}, bf16[128]{0:T(256)(128)(2,1)}, u32[]{:S(2)}) copy-start(bf16[128]{0:T(256)(128)(2,1)} %param.13) | copy-start | bytes 772
  19.1 3.2 %collective-permute-start.6 = (bf16[2,2,4,16,128]{4,3,2,1,0:T(8,128)(2,1)S(1)}, bf16[2,2,4,16,128]{4,3,2,1,0:T(8,128)(2,1)S(1)}, u32[]{:S(2)}, u32[]{:S(2)}) collective-permute-start(bf16[2,2,4,16,128]{4,3,2,1,0:T(8,128)(2,1)S(1)} %get-tuple-element.52), channel_id=1, source_target_pairs={{0,8},{4,12},{8,0},{12,4},{16,24},{20,28},{24,16},{28,20},{1,9},{5... | collective-permute-start | bytes 196616 | tf_op jit(solution)/shard_map/ppermute | solution.py:298
  20.1 3.1 %collective-permute-start.7 = (bf16[2,2,4,16,128]{4,3,2,1,0:T(8,128)(2,1)S(1)}, bf16[2,2,4,16,128]{4,3,2,1,0:T(8,128)(2,1)S(1)}, u32[]{:S(2)}, u32[]{:S(2)}) collective-permute-start(bf16[2,2,4,16,128]{4,3,2,1,0:T(8,128)(2,1)S(1)} %get-tuple-element.53), channel_id=1, source_target_pairs={{0,16},{4,20},{8,24},{12,28},{16,0},{20,4},{24,8},{28,12},{1,17},{... | collective-permute-start | bytes 196616 | tf_op jit(solution)/shard_map/ppermute | solution.py:298
  20.4 4.0 %collective-permute-start.8 = (bf16[2,2,4,16,128]{4,3,2,1,0:T(8,128)(2,1)S(1)}, bf16[2,2,4,16,128]{4,3,2,1,0:T(8,128)(2,1)S(1)}, u32[]{:S(2)}, u32[]{:S(2)}) collective-permute-start(bf16[2,2,4,16,128]{4,3,2,1,0:T(8,128)(2,1)S(1)} %get-tuple-element.54), channel_id=1, source_target_pairs={{0,24},{4,28},{8,16},{12,20},{16,8},{20,12},{24,0},{28,4},{1,25},{... | collective-permute-start | bytes 196616 | tf_op jit(solution)/shard_map/ppermute | solution.py:298
  24.5 6.5 %collective-permute-start.9 = (bf16[4,2,4,16,128]{4,3,2,1,0:T(8,128)(2,1)S(1)}, bf16[4,2,4,16,128]{4,3,2,1,0:T(8,128)(2,1)S(1)}, u32[]{:S(2)}, u32[]{:S(2)}) collective-permute-start(bf16[4,2,4,16,128]{4,3,2,1,0:T(8,128)(2,1)S(1)} %pad_maximum_fusion.2), channel_id=1, source_target_pairs={{0,4},{4,0},{8,12},{12,8},{16,20},{20,16},{24,28},{28,24},{1,5},{5... | collective-permute-start | bytes 393224 | tf_op jit(solution)/shard_map/ppermute | solution.py:298
